TPU v7x, 256 devices: a whole 4x4x8 slice. The times are simulated.
256 devices in a mesh: blk: 128 (over x_lo, z, y, core), rep: 2 (over x_hi).
Axes of the slice: x: 4 (x_hi: 2, x_lo: 2; x = x_hi * 2 + x_lo), y: 4, z: 8, core: 2. Of those that a mesh axis runs over, the one named last changes fastest.
Arguments:
- factors: float32 [128, 2, 300, 512], P('blk', None, 'rep'), may hold values from -1.5 to 1.5
- state: float32 [128, 2, 300, 512], P('blk', None, 'rep'), may hold values from 30 to 3000
- counts: int32 [128, 8, 512, 512], P('blk'), may hold values from 0 to 1024, as said below
Outputs:
- step: float32 [128, 2, 300, 512], P('blk', None, 'rep')
- new_state: float32 [128, 2, 300, 512], P('blk', None, 'rep')
Inputs may be any that keep to these rules, and one draw needn't show every extreme that they name: counts[p, r] is the tile of the two blocks that meet at player p in round r, and each pair of blocks meets at most once in the 8 rounds.
All inputs are finite; a program needn't handle non-finite values.
Results may differ from a plain program's by a relative error of at most 0.0003.
Values sent between devices are 32-bit elements; how exact they have to be, the bound alone decides.
A program may use at most 128 MiB of HBM per device.

v0:
```python
import jax
import jax.numpy as jnp
from jax import lax
from jax.sharding import PartitionSpec as P

clip_bound = 2.0


def from_behind(block, axis, distance):
    devices = range(lax.axis_size(axis))
    route = [(i - distance, i) for i in devices if i - distance in devices]
    return lax.ppermute(block, axis, route)


def joined_along(blocks, dim):
    blocks = jnp.moveaxis(blocks, 0, dim)
    dims = blocks.shape
    return blocks.reshape(*dims[:dim], dims[dim] * dims[dim + 1], *dims[dim + 2 :])


def from_everyone(value, axis):
    copies = jnp.broadcast_to(value, (lax.axis_size(axis), *value.shape))
    return lax.all_to_all(copies, axis, split_axis=0, concat_axis=0, tiled=True)


def gathered_copies(value, axis, dim):
    return joined_along(from_everyone(value, axis), dim)


def split_up(value, dim, peers):
    before, after = (value.shape[:dim], value.shape[dim + 1 :])
    return jnp.moveaxis(value.reshape(*before, peers, -1, *after), dim, 0)


def sent_and_summed(value, axis, dim):
    peers = lax.axis_size(axis)
    blocks = lax.all_to_all(split_up(value, dim, peers), axis, 0, 0, tiled=True)
    return jnp.sum(blocks, axis=0)


def residual_of(scores, count_tile):
    amount = count_tile.astype(jnp.float32)
    present = count_tile > 0
    clamped = jnp.maximum(amount, 1.0)
    weight = 0.1 + 0.25 * jnp.sqrt(clamped)
    kept = weight * jnp.clip(scores - jnp.log(clamped), -clip_bound, clip_bound)
    return jnp.where(present, kept, 0.5 * jax.nn.sigmoid(scores))


def inner_first(left, right):
    return lax.dot_general(
        left,
        right,
        (((0,), (0,)), ((), ())),
        precision=lax.Precision.HIGHEST,
        preferred_element_type=jnp.float32,
    )


def product(left, right):
    return jnp.dot(left, right, precision=lax.Precision.HIGHEST, preferred_element_type=jnp.float32)


def meeting(upper_block, lower_block, count_tile):
    items = upper_block.shape[1]
    share_rows = items // lax.axis_size("rep")
    offset = lax.axis_index("rep") * share_rows
    upper_rows = lax.dynamic_slice_in_dim(upper_block, offset, share_rows, 1)
    tile_rows = lax.dynamic_slice_in_dim(count_tile, offset, share_rows, 0)
    residual = residual_of(inner_first(upper_rows, lower_block), tile_rows)
    grad_part = lax.dot_general(
        lower_block,
        residual,
        (((1,), (1,)), ((), ())),
        precision=lax.Precision.HIGHEST,
        preferred_element_type=jnp.float32,
    )
    grad_upper = lax.dynamic_update_slice_in_dim(jnp.zeros_like(upper_block), grad_part, offset, 1)
    grad_lower = product(upper_rows, residual)
    return (grad_upper, grad_lower)


def rotate(upper_stack, lower_stack, player, finish):
    outgoing = jnp.where(player == 0, lower_stack, upper_stack)
    arrived_up = from_behind(outgoing, "blk", 1)
    arrived_down = from_behind(lower_stack, "blk", -1)
    new_upper = jnp.where(player == 0, upper_stack, arrived_up)
    new_lower = jnp.where(player == finish, upper_stack, arrived_down)
    return (new_upper, new_lower)


def return_home(acc_upper, acc_lower, player, finish):
    from_next = from_behind(acc_upper, "blk", -1)
    from_prior = from_behind(acc_lower, "blk", 1)
    old_upper = jnp.where(player == 0, acc_upper, jnp.where(player == finish, acc_lower, from_next))
    old_lower = jnp.where(player == 0, from_next, from_prior)
    return (old_upper, old_lower)


def body(factors, state, counts):
    player = lax.axis_index("blk")
    finish = lax.axis_size("blk") - 1
    rounds = counts.shape[1]
    whole = gathered_copies(factors, "rep", 2)
    upper_block = whole[0, 0]
    lower_block = whole[0, 1]
    pieces = []
    for turn in range(rounds):
        grad_upper, grad_lower = meeting(upper_block, lower_block, counts[0, turn])
        pieces.append((grad_upper, grad_lower))
        if turn < rounds - 1:
            upper_block, lower_block = rotate(upper_block, lower_block, player, finish)
    acc_upper, acc_lower = pieces[rounds - 1]
    for turn in range(rounds - 2, -1, -1):
        acc_upper, acc_lower = return_home(acc_upper, acc_lower, player, finish)
        acc_upper = acc_upper + pieces[turn][0]
        acc_lower = acc_lower + pieces[turn][1]
    stacked = jnp.stack([acc_upper, acc_lower])[None]
    grad = sent_and_summed(stacked, "rep", 2)
    new_state = state + grad * grad
    step = grad / jnp.sqrt(new_state)
    return (step, new_state)


def solution(mesh):
    in_specs = (
        P("blk", None, "rep", None),
        P("blk", None, "rep", None),
        P("blk", None, None, None),
    )
    out_specs = (P("blk", None, "rep", None), P("blk", None, "rep", None))
    return jax.shard_map(body, mesh=mesh, in_specs=in_specs, out_specs=out_specs, check_vma=False)
```

profile of v0, /device:TPU:2, one launch (start us, length us, event | category | flops | bytes accessed | tf_op | source)
XLA Modules:
  0.0 337.9 jit_solution(2439452863358652168)
XLA Ops:
  6.7 17.3 %all-to-all-done = f32[2,1,2,150,512]{4,2,3,1,0:T(2,128)S(1)} async-done(((f32[2,1,2,150,512]{4,2,3,1,0:T(2,128)}), f32[2,1,2,150,512]{4,2,3,1,0:T(2,128)S(1)}, u32[]{:S(2)}, u32[]{:S(2)}) %all-to-all-start) | async-done | bytes 1228832 | tf_op jit(solution)/shard_map/all_to_all | solution.py:23
  27.9 8.9 %collective-permute-start.1 = (f32[300,512]{1,0:T(8,128)S(1)}, f32[300,512]{1,0:T(8,128)S(1)}, u32[]{:S(2)}, u32[]{:S(2)}) collective-permute-start(f32[300,512]{1,0:T(8,128)S(1)} %bitcast.169), channel_id=1, source_target_pairs={{2,0},{4,2},{6,4},{8,6},{10,8},{12,10},{14,12},{16,14},{18,16},{20... | collective-permute-start | bytes 1843208 | tf_op jit(solution)/shard_map/ppermute | solution.py:12
  36.8 6.2 %collective-permute-done = f32[300,512]{1,0:T(8,128)S(1)} collective-permute-done((f32[300,512]{1,0:T(8,128)}, f32[300,512]{1,0:T(8,128)S(1)}, u32[]{:S(2)}, u32[]{:S(2)}) %collective-permute-start) | collective-permute-done | bytes 614432 | tf_op jit(solution)/shard_map/ppermute | solution.py:12
  44.7 8.0 %collective-permute-start.3 = (f32[300,512]{1,0:T(8,128)S(1)}, f32[300,512]{1,0:T(8,128)S(1)}, u32[]{:S(2)}, u32[]{:S(2)}) collective-permute-start(f32[300,512]{1,0:T(8,128)S(1)} %get-tuple-element.20), channel_id=1, source_target_pairs={{2,0},{4,2},{6,4},{8,6},{10,8},{12,10},{14,12},{16,14},{18,16},{20... | collective-permute-start | bytes 1843208 | tf_op jit(solution)/shard_map/ppermute | solution.py:12
  60.5 8.0 %collective-permute-done.2 = f32[300,512]{1,0:T(8,128)S(1)} collective-permute-done((f32[300,512]{1,0:T(8,128)S(1)}, f32[300,512]{1,0:T(8,128)S(1)}, u32[]{:S(2)}, u32[]{:S(2)}) %collective-permute-start.2) | collective-permute-done | bytes 614432 | tf_op jit(solution)/shard_map/ppermute | solution.py:12
  70.7 7.9 %collective-permute-start.5 = (f32[300,512]{1,0:T(8,128)S(1)}, f32[300,512]{1,0:T(8,128)S(1)}, u32[]{:S(2)}, u32[]{:S(2)}) collective-permute-start(f32[300,512]{1,0:T(8,128)S(1)} %get-tuple-element.17), channel_id=1, source_target_pairs={{2,0},{4,2},{6,4},{8,6},{10,8},{12,10},{14,12},{16,14},{18,16},{20... | collective-permute-start | bytes 1843208 | tf_op jit(solution)/shard_map/ppermute | solution.py:12
  78.6 6.0 %collective-permute-done.4 = f32[300,512]{1,0:T(8,128)S(1)} collective-permute-done((f32[300,512]{1,0:T(8,128)S(1)}, f32[300,512]{1,0:T(8,128)S(1)}, u32[]{:S(2)}, u32[]{:S(2)}) %collective-permute-start.4) | collective-permute-done | bytes 614432 | tf_op jit(solution)/shard_map/ppermute | solution.py:12
  88.5 8.0 %collective-permute-start.7 = (f32[300,512]{1,0:T(8,128)S(1)}, f32[300,512]{1,0:T(8,128)S(1)}, u32[]{:S(2)}, u32[]{:S(2)}) collective-permute-start(f32[300,512]{1,0:T(8,128)S(1)} %get-tuple-element.14), channel_id=1, source_target_pairs={{2,0},{4,2},{6,4},{8,6},{10,8},{12,10},{14,12},{16,14},{18,16},{20... | collective-permute-start | bytes 1843208 | tf_op jit(solution)/shard_map/ppermute | solution.py:12
  96.6 6.0 %collective-permute-done.6 = f32[300,512]{1,0:T(8,128)S(1)} collective-permute-done((f32[300,512]{1,0:T(8,128)S(1)}, f32[300,512]{1,0:T(8,128)S(1)}, u32[]{:S(2)}, u32[]{:S(2)}) %collective-permute-start.6) | collective-permute-done | bytes 614432 | tf_op jit(solution)/shard_map/ppermute | solution.py:12
  106.5 8.0 %collective-permute-start.9 = (f32[300,512]{1,0:T(8,128)S(1)}, f32[300,512]{1,0:T(8,128)S(1)}, u32[]{:S(2)}, u32[]{:S(2)}) collective-permute-start(f32[300,512]{1,0:T(8,128)S(1)} %get-tuple-element.11), channel_id=1, source_target_pairs={{2,0},{4,2},{6,4},{8,6},{10,8},{12,10},{14,12},{16,14},{18,16},{20... | collective-permute-start | bytes 1843208 | tf_op jit(solution)/shard_map/ppermute | solution.py:12
  114.6 6.0 %collective-permute-done.8 = f32[300,512]{1,0:T(8,128)S(1)} collective-permute-done((f32[300,512]{1,0:T(8,128)S(1)}, f32[300,512]{1,0:T(8,128)S(1)}, u32[]{:S(2)}, u32[]{:S(2)}) %collective-permute-start.8) | collective-permute-done | bytes 614432 | tf_op jit(solution)/shard_map/ppermute | solution.py:12
  124.5 8.0 %collective-permute-start.11 = (f32[300,512]{1,0:T(8,128)S(1)}, f32[300,512]{1,0:T(8,128)S(1)}, u32[]{:S(2)}, u32[]{:S(2)}) collective-permute-start(f32[300,512]{1,0:T(8,128)S(1)} %get-tuple-element.8), channel_id=1, source_target_pairs={{2,0},{4,2},{6,4},{8,6},{10,8},{12,10},{14,12},{16,14},{18,16},{20... | collective-permute-start | bytes 1843208 | tf_op jit(solution)/shard_map/ppermute | solution.py:12
  132.6 6.0 %collective-permute-done.10 = f32[300,512]{1,0:T(8,128)S(1)} collective-permute-done((f32[300,512]{1,0:T(8,128)S(1)}, f32[300,512]{1,0:T(8,128)S(1)}, u32[]{:S(2)}, u32[]{:S(2)}) %collective-permute-start.10) | collective-permute-done | bytes 614432 | tf_op jit(solution)/shard_map/ppermute | solution.py:12
  141.6 8.0 %collective-permute-start.12 = (f32[300,512]{1,0:T(8,128)}, f32[300,512]{1,0:T(8,128)}, u32[]{:S(2)}, u32[]{:S(2)}) collective-permute-start(f32[300,512]{1,0:T(8,128)} %get-tuple-element.5), channel_id=1, source_target_pairs={{2,0},{4,2},{6,4},{8,6},{10,8},{12,10},{14,12},{16,14},{18,16},{20... | collective-permute-start | bytes 1843208 | tf_op jit(solution)/shard_map/ppermute | solution.py:12
  157.7 8.0 %collective-permute-done.13 = f32[300,512]{1,0:T(8,128)} collective-permute-done((f32[300,512]{1,0:T(8,128)}, f32[300,512]{1,0:T(8,128)}, u32[]{:S(2)}, u32[]{:S(2)}) %collective-permute-start.13) | collective-permute-done | bytes 614432 | tf_op jit(solution)/shard_map/ppermute | solution.py:12
  183.3 8.0 %collective-permute-start.16 = (f32[300,512]{1,0:T(8,128)S(1)}, f32[300,512]{1,0:T(8,128)S(1)}, u32[]{:S(2)}, u32[]{:S(2)}) collective-permute-start(f32[300,512]{1,0:T(8,128)S(1)} %add_dynamic-update-slice_fusion.5), channel_id=1, source_target_pairs={{2,0},{4,2},{6,4},{8,6},{10,8},{12,10},{14,12},{16,14},{18,16},{20... | collective-permute-start | bytes 1843208 | tf_op jit(solution)/shard_map/ppermute | solution.py:12
  199.1 8.0 %collective-permute-done.15 = f32[300,512]{1,0:T(8,128)S(1)} collective-permute-done((f32[300,512]{1,0:T(8,128)S(1)}, f32[300,512]{1,0:T(8,128)S(1)}, u32[]{:S(2)}, u32[]{:S(2)}) %collective-permute-start.15) | collective-permute-done | bytes 614432 | tf_op jit(solution)/shard_map/ppermute | solution.py:12
  218.3 8.0 %collective-permute-done.17 = f32[300,512]{1,0:T(8,128)S(1)} collective-permute-done((f32[300,512]{1,0:T(8,128)S(1)}, f32[300,512]{1,0:T(8,128)S(1)}, u32[]{:S(2)}, u32[]{:S(2)}) %collective-permute-start.17) | collective-permute-done | bytes 614432 | tf_op jit(solution)/shard_map/ppermute | solution.py:12
  237.5 8.0 %collective-permute-done.19 = f32[300,512]{1,0:T(8,128)S(1)} collective-permute-done((f32[300,512]{1,0:T(8,128)S(1)}, f32[300,512]{1,0:T(8,128)S(1)}, u32[]{:S(2)}, u32[]{:S(2)}) %collective-permute-start.19) | collective-permute-done | bytes 614432 | tf_op jit(solution)/shard_map/ppermute | solution.py:12
  256.7 8.0 %collective-permute-done.21 = f32[300,512]{1,0:T(8,128)S(1)} collective-permute-done((f32[300,512]{1,0:T(8,128)S(1)}, f32[300,512]{1,0:T(8,128)S(1)}, u32[]{:S(2)}, u32[]{:S(2)}) %collective-permute-start.21) | collective-permute-done | bytes 614432 | tf_op jit(solution)/shard_map/ppermute | solution.py:12
  275.9 8.3 %collective-permute-done.23 = f32[300,512]{1,0:T(8,128)S(1)} collective-permute-done((f32[300,512]{1,0:T(8,128)S(1)}, f32[300,512]{1,0:T(8,128)S(1)}, u32[]{:S(2)}, u32[]{:S(2)}) %collective-permute-start.23) | collective-permute-done | bytes 614432 | tf_op jit(solution)/shard_map/ppermute | solution.py:12
  289.0 7.9 %collective-permute-start.26 = (f32[300,512]{1,0:T(8,128)S(1)}, f32[300,512]{1,0:T(8,128)S(1)}, u32[]{:S(2)}, u32[]{:S(2)}) collective-permute-start(f32[300,512]{1,0:T(8,128)S(1)} %add_dynamic-update-slice_fusion), channel_id=1, source_target_pairs={{2,0},{4,2},{6,4},{8,6},{10,8},{12,10},{14,12},{16,14},{18,16},{20... | collective-permute-start | bytes 1843208 | tf_op jit(solution)/shard_map/ppermute | solution.py:12
  305.7 11.7 %collective-permute-done.27 = f32[300,512]{1,0:T(8,128)S(1)} collective-permute-done((f32[300,512]{1,0:T(8,128)S(1)}, f32[300,512]{1,0:T(8,128)S(1)}, u32[]{:S(2)}, u32[]{:S(2)}) %collective-permute-start.27) | collective-permute-done | bytes 614432 | tf_op jit(solution)/shard_map/ppermute | solution.py:12
  319.7 14.3 %all_to_all.10 = f32[2,1,2,150,512]{4,2,3,1,0:T(2,128)S(1)} all-to-all(f32[2,1,2,150,512]{4,2,3,1,0:T(2,128)S(1)} %copy.8), channel_id=1, replica_groups=mesh['blk'=128,'rep'=2] {'rep'}, dimensions={0} | all-to-all | bytes 2457600 | tf_op jit(solution)/shard_map/all_to_all | solution.py:37
  (116 shorter events, 133.7 us)
Async XLA Ops:
  3.1 20.9 %all-to-all-start = ((f32[2,1,2,150,512]{4,2,3,1,0:T(2,128)}), f32[2,1,2,150,512]{4,2,3,1,0:T(2,128)S(1)}, u32[]{:S(2)}, u32[]{:S(2)}) async-start(f32[2,1,2,150,512]{4,2,3,1,0:T(2,128)} %broadcast_in_dim.3), calls=%async_computation | async-start | bytes 2457600 | tf_op jit(solution)/shard_map/all_to_all | solution.py:23
  26.0 17.0 %collective-permute-start = (f32[300,512]{1,0:T(8,128)}, f32[300,512]{1,0:T(8,128)S(1)}, u32[]{:S(2)}, u32[]{:S(2)}) collective-permute-start(f32[300,512]{1,0:T(8,128)} %bitcast_select_fusion.2), channel_id=1, source_target_pairs={{0,2},{2,4},{4,6},{6,8},{8,10},{10,12},{12,14},{14,16},{16,18},{18... | collective-permute-start | bytes 1843208 | tf_op jit(solution)/shard_map/ppermute | solution.py:12
  27.9 16.6 %collective-permute-start.1 = (f32[300,512]{1,0:T(8,128)S(1)}, f32[300,512]{1,0:T(8,128)S(1)}, u32[]{:S(2)}, u32[]{:S(2)}) collective-permute-start(f32[300,512]{1,0:T(8,128)S(1)} %bitcast.169), channel_id=1, source_target_pairs={{2,0},{4,2},{6,4},{8,6},{10,8},{12,10},{14,12},{16,14},{18,16},{20... | collective-permute-start | bytes 1843208 | tf_op jit(solution)/shard_map/ppermute | solution.py:12
  44.7 15.8 %collective-permute-start.3 = (f32[300,512]{1,0:T(8,128)S(1)}, f32[300,512]{1,0:T(8,128)S(1)}, u32[]{:S(2)}, u32[]{:S(2)}) collective-permute-start(f32[300,512]{1,0:T(8,128)S(1)} %get-tuple-element.20), channel_id=1, source_target_pairs={{2,0},{4,2},{6,4},{8,6},{10,8},{12,10},{14,12},{16,14},{18,16},{20... | collective-permute-start | bytes 1843208 | tf_op jit(solution)/shard_map/ppermute | solution.py:12
  52.8 15.8 %collective-permute-start.2 = (f32[300,512]{1,0:T(8,128)S(1)}, f32[300,512]{1,0:T(8,128)S(1)}, u32[]{:S(2)}, u32[]{:S(2)}) collective-permute-start(f32[300,512]{1,0:T(8,128)S(1)} %get-tuple-element.19), channel_id=1, source_target_pairs={{0,2},{2,4},{4,6},{6,8},{8,10},{10,12},{12,14},{14,16},{16,18},{18... | collective-permute-start | bytes 1843208 | tf_op jit(solution)/shard_map/ppermute | solution.py:12
  68.8 15.8 %collective-permute-start.4 = (f32[300,512]{1,0:T(8,128)S(1)}, f32[300,512]{1,0:T(8,128)S(1)}, u32[]{:S(2)}, u32[]{:S(2)}) collective-permute-start(f32[300,512]{1,0:T(8,128)S(1)} %get-tuple-element.16), channel_id=1, source_target_pairs={{0,2},{2,4},{4,6},{6,8},{8,10},{10,12},{12,14},{14,16},{16,18},{18... | collective-permute-start | bytes 1843208 | tf_op jit(solution)/shard_map/ppermute | solution.py:12
  70.7 15.6 %collective-permute-start.5 = (f32[300,512]{1,0:T(8,128)S(1)}, f32[300,512]{1,0:T(8,128)S(1)}, u32[]{:S(2)}, u32[]{:S(2)}) collective-permute-start(f32[300,512]{1,0:T(8,128)S(1)} %get-tuple-element.17), channel_id=1, source_target_pairs={{2,0},{4,2},{6,4},{8,6},{10,8},{12,10},{14,12},{16,14},{18,16},{20... | collective-permute-start | bytes 1843208 | tf_op jit(solution)/shard_map/ppermute | solution.py:12
  86.6 15.9 %collective-permute-start.6 = (f32[300,512]{1,0:T(8,128)S(1)}, f32[300,512]{1,0:T(8,128)S(1)}, u32[]{:S(2)}, u32[]{:S(2)}) collective-permute-start(f32[300,512]{1,0:T(8,128)S(1)} %get-tuple-element.13), channel_id=1, source_target_pairs={{0,2},{2,4},{4,6},{6,8},{8,10},{10,12},{12,14},{14,16},{16,18},{18... | collective-permute-start | bytes 1843208 | tf_op jit(solution)/shard_map/ppermute | solution.py:12
  88.5 15.8 %collective-permute-start.7 = (f32[300,512]{1,0:T(8,128)S(1)}, f32[300,512]{1,0:T(8,128)S(1)}, u32[]{:S(2)}, u32[]{:S(2)}) collective-permute-start(f32[300,512]{1,0:T(8,128)S(1)} %get-tuple-element.14), channel_id=1, source_target_pairs={{2,0},{4,2},{6,4},{8,6},{10,8},{12,10},{14,12},{16,14},{18,16},{20... | collective-permute-start | bytes 1843208 | tf_op jit(solution)/shard_map/ppermute | solution.py:12
  104.6 15.9 %collective-permute-start.8 = (f32[300,512]{1,0:T(8,128)S(1)}, f32[300,512]{1,0:T(8,128)S(1)}, u32[]{:S(2)}, u32[]{:S(2)}) collective-permute-start(f32[300,512]{1,0:T(8,128)S(1)} %get-tuple-element.10), channel_id=1, source_target_pairs={{0,2},{2,4},{4,6},{6,8},{8,10},{10,12},{12,14},{14,16},{16,18},{18... | collective-permute-start | bytes 1843208 | tf_op jit(solution)/shard_map/ppermute | solution.py:12
  106.5 15.8 %collective-permute-start.9 = (f32[300,512]{1,0:T(8,128)S(1)}, f32[300,512]{1,0:T(8,128)S(1)}, u32[]{:S(2)}, u32[]{:S(2)}) collective-permute-start(f32[300,512]{1,0:T(8,128)S(1)} %get-tuple-element.11), channel_id=1, source_target_pairs={{2,0},{4,2},{6,4},{8,6},{10,8},{12,10},{14,12},{16,14},{18,16},{20... | collective-permute-start | bytes 1843208 | tf_op jit(solution)/shard_map/ppermute | solution.py:12
  122.6 15.9 %collective-permute-start.10 = (f32[300,512]{1,0:T(8,128)S(1)}, f32[300,512]{1,0:T(8,128)S(1)}, u32[]{:S(2)}, u32[]{:S(2)}) collective-permute-start(f32[300,512]{1,0:T(8,128)S(1)} %get-tuple-element.7), channel_id=1, source_target_pairs={{0,2},{2,4},{4,6},{6,8},{8,10},{10,12},{12,14},{14,16},{16,18},{18... | collective-permute-start | bytes 1843208 | tf_op jit(solution)/shard_map/ppermute | solution.py:12
  124.5 15.8 %collective-permute-start.11 = (f32[300,512]{1,0:T(8,128)S(1)}, f32[300,512]{1,0:T(8,128)S(1)}, u32[]{:S(2)}, u32[]{:S(2)}) collective-permute-start(f32[300,512]{1,0:T(8,128)S(1)} %get-tuple-element.8), channel_id=1, source_target_pairs={{2,0},{4,2},{6,4},{8,6},{10,8},{12,10},{14,12},{16,14},{18,16},{20... | collective-permute-start | bytes 1843208 | tf_op jit(solution)/shard_map/ppermute | solution.py:12
  141.6 16.1 %collective-permute-start.12 = (f32[300,512]{1,0:T(8,128)}, f32[300,512]{1,0:T(8,128)}, u32[]{:S(2)}, u32[]{:S(2)}) collective-permute-start(f32[300,512]{1,0:T(8,128)} %get-tuple-element.5), channel_id=1, source_target_pairs={{2,0},{4,2},{6,4},{8,6},{10,8},{12,10},{14,12},{16,14},{18,16},{20... | collective-permute-start | bytes 1843208 | tf_op jit(solution)/shard_map/ppermute | solution.py:12
  149.6 16.1 %collective-permute-start.13 = (f32[300,512]{1,0:T(8,128)}, f32[300,512]{1,0:T(8,128)}, u32[]{:S(2)}, u32[]{:S(2)}) collective-permute-start(f32[300,512]{1,0:T(8,128)} %get-tuple-element.4), channel_id=1, source_target_pairs={{0,2},{2,4},{4,6},{6,8},{8,10},{10,12},{12,14},{14,16},{16,18},{18... | collective-permute-start | bytes 1843208 | tf_op jit(solution)/shard_map/ppermute | solution.py:12
  183.3 15.8 %collective-permute-start.16 = (f32[300,512]{1,0:T(8,128)S(1)}, f32[300,512]{1,0:T(8,128)S(1)}, u32[]{:S(2)}, u32[]{:S(2)}) collective-permute-start(f32[300,512]{1,0:T(8,128)S(1)} %add_dynamic-update-slice_fusion.5), channel_id=1, source_target_pairs={{2,0},{4,2},{6,4},{8,6},{10,8},{12,10},{14,12},{16,14},{18,16},{20... | collective-permute-start | bytes 1843208 | tf_op jit(solution)/shard_map/ppermute | solution.py:12
  191.4 15.8 %collective-permute-start.15 = (f32[300,512]{1,0:T(8,128)S(1)}, f32[300,512]{1,0:T(8,128)S(1)}, u32[]{:S(2)}, u32[]{:S(2)}) collective-permute-start(f32[300,512]{1,0:T(8,128)S(1)} %get-tuple-element.37), channel_id=1, source_target_pairs={{0,2},{2,4},{4,6},{6,8},{8,10},{10,12},{12,14},{14,16},{16,18},{18... | collective-permute-start | bytes 1843208 | tf_op jit(solution)/shard_map/ppermute | solution.py:12
  210.6 15.8 %collective-permute-start.17 = (f32[300,512]{1,0:T(8,128)S(1)}, f32[300,512]{1,0:T(8,128)S(1)}, u32[]{:S(2)}, u32[]{:S(2)}) collective-permute-start(f32[300,512]{1,0:T(8,128)S(1)} %get-tuple-element.39), channel_id=1, source_target_pairs={{0,2},{2,4},{4,6},{6,8},{8,10},{10,12},{12,14},{14,16},{16,18},{18... | collective-permute-start | bytes 1843208 | tf_op jit(solution)/shard_map/ppermute | solution.py:12
  229.8 15.8 %collective-permute-start.19 = (f32[300,512]{1,0:T(8,128)S(1)}, f32[300,512]{1,0:T(8,128)S(1)}, u32[]{:S(2)}, u32[]{:S(2)}) collective-permute-start(f32[300,512]{1,0:T(8,128)S(1)} %get-tuple-element.41), channel_id=1, source_target_pairs={{0,2},{2,4},{4,6},{6,8},{8,10},{10,12},{12,14},{14,16},{16,18},{18... | collective-permute-start | bytes 1843208 | tf_op jit(solution)/shard_map/ppermute | solution.py:12
  249.0 15.8 %collective-permute-start.21 = (f32[300,512]{1,0:T(8,128)S(1)}, f32[300,512]{1,0:T(8,128)S(1)}, u32[]{:S(2)}, u32[]{:S(2)}) collective-permute-start(f32[300,512]{1,0:T(8,128)S(1)} %get-tuple-element.43), channel_id=1, source_target_pairs={{0,2},{2,4},{4,6},{6,8},{8,10},{10,12},{12,14},{14,16},{16,18},{18... | collective-permute-start | bytes 1843208 | tf_op jit(solution)/shard_map/ppermute | solution.py:12
  268.2 16.0 %collective-permute-start.23 = (f32[300,512]{1,0:T(8,128)S(1)}, f32[300,512]{1,0:T(8,128)S(1)}, u32[]{:S(2)}, u32[]{:S(2)}) collective-permute-start(f32[300,512]{1,0:T(8,128)S(1)} %get-tuple-element.45), channel_id=1, source_target_pairs={{0,2},{2,4},{4,6},{6,8},{8,10},{10,12},{12,14},{14,16},{16,18},{18... | collective-permute-start | bytes 1843208 | tf_op jit(solution)/shard_map/ppermute | solution.py:12
  285.0 15.9 %collective-permute-start.25 = (f32[300,512]{1,0:T(8,128)S(1)}, f32[300,512]{1,0:T(8,128)S(1)}, u32[]{:S(2)}, u32[]{:S(2)}) collective-permute-start(f32[300,512]{1,0:T(8,128)S(1)} %get-tuple-element.47), channel_id=1, source_target_pairs={{0,2},{2,4},{4,6},{6,8},{8,10},{10,12},{12,14},{14,16},{16,18},{18... | collective-permute-start | bytes 1843208 | tf_op jit(solution)/shard_map/ppermute | solution.py:12
  289.0 16.7 %collective-permute-start.26 = (f32[300,512]{1,0:T(8,128)S(1)}, f32[300,512]{1,0:T(8,128)S(1)}, u32[]{:S(2)}, u32[]{:S(2)}) collective-permute-start(f32[300,512]{1,0:T(8,128)S(1)} %add_dynamic-update-slice_fusion), channel_id=1, source_target_pairs={{2,0},{4,2},{6,4},{8,6},{10,8},{12,10},{14,12},{16,14},{18,16},{20... | collective-permute-start | bytes 1843208 | tf_op jit(solution)/shard_map/ppermute | solution.py:12
  301.6 15.8 %collective-permute-start.27 = (f32[300,512]{1,0:T(8,128)S(1)}, f32[300,512]{1,0:T(8,128)S(1)}, u32[]{:S(2)}, u32[]{:S(2)}) collective-permute-start(f32[300,512]{1,0:T(8,128)S(1)} %select_add_fusion.1), channel_id=1, source_target_pairs={{0,2},{2,4},{4,6},{6,8},{8,10},{10,12},{12,14},{14,16},{16,18},{18... | collective-permute-start | bytes 1843208 | tf_op jit(solution)/shard_map/ppermute | solution.py:12
  (22 other events, 269.3 us)
where the time goes:
time: 339 us; the launch traced here: 338 us
  waiting for transfers between devices  162 us (48%)
  starting transfers between devices  115 us (34%)
  matrix products  27.9 us (8%)
  blocking collectives  14.3 us (4%)
  local copies, waits for them, and re-layouts  11.8 us (3%)
  other arithmetic  5.13 us (2%)
    ppermute x28, waiting for transfers between devices, from_behind(): return lax.ppermute(block, axis, route)  145 us
    ppermute x28, starting transfers between devices, from_behind(): return lax.ppermute(block, axis, route)  112 us
    all_to_all x1, waiting for transfers between devices, from_everyone(): return lax.all_to_all(copies, axis, split_axis=0, concat_axis=0, tiled=True)  17.3 us
    all_to_all x1, blocking collectives, sent_and_summed(): blocks = lax.all_to_all(split_up(value, dim, peers), axis, 0, 0, tiled=True)  14.3 us
    dot_general x8, matrix products, inner_first(): lax.dot_general(left, right, (((0,), (0,)), ((), ())), precision=lax.Prec...  13.1 us
    dot_general x8, matrix products, meeting(): lax.dot_general(lower_block, residual, (((1,), (1,)), ((), ())), precisio...  7.83 us
    dot_general x8, matrix products, product(): jnp.dot(left, right, precision=lax.Precision.HIGHEST, preferred_element_t...  7.02 us
  transfers between devices with their start and end apart: 29, of which 28 were waited for; matrix products, arithmetic and copies ran while one was open for 5% of the time, Pallas kernels for 0%

commit v1 on v0

v1 whole, which is shorter than its diff:
```python
import functools

import jax
import jax.numpy as jnp
from jax import lax
from jax.experimental import pallas as pl
from jax.experimental.pallas import tpu as pltpu
from jax.sharding import PartitionSpec as P

MESH = pl.DeviceIdType.MESH
BF16 = jnp.bfloat16
F32 = jnp.float32
clip_bound = 2.0

A_AT, B_AT, FIXED, SLOTS = 0, 4, 9, 10


def residual_of(scores, count_tile):
    amount = count_tile.astype(F32)
    present = count_tile > 0
    clamped = jnp.maximum(amount, 1.0)
    weight = 0.1 + 0.25 * jnp.sqrt(clamped)
    kept = weight * jnp.clip(scores - jnp.log(clamped), -clip_bound, clip_bound)
    return jnp.where(present, kept, 0.5 * jax.nn.sigmoid(scores))


def split(value):
    high = value.astype(BF16)
    return high, (value - high.astype(F32)).astype(BF16)


def dot3(left, right, dims):
    (lh, ll), (rh, rl) = left, right

    def one(a, b):
        return lax.dot_general(a, b, (dims, ((), ())), preferred_element_type=F32)

    return one(lh, rh) + one(lh, rl) + one(ll, rh)


def kernel(
    chips, tile, factors, counts, out,
    x, g, from_core, from_chain, swapped, extra, tiles, uh, ul, lh, ll,
    load_sem, count_sem,
    in_send, in_recv, fix_send, fix_recv,
    chain_send, chain_recv, core_send, core_recv,
    gcore_send, gcore_recv, gchain_send, gchain_recv,
    out_send, out_recv, gfix_send, gfix_recv,
):
    p, q = lax.axis_index("blk"), lax.axis_index("rep")
    c, h = p // 2, p % 2
    differs = (h + q) % 2
    same = differs == 0
    other = differs == 1
    first = c == 0
    sibling = (c * 2 + 1 - h, q)
    partner = (c * 2 + 1 - h, 1 - q)
    at_end = c == chips - 1
    right = (jnp.where(at_end, c, c + 1) * 2 + h, jnp.where(at_end, 1 - q, q))
    left = (jnp.maximum(c - 1, 0) * 2 + h, q)
    even = q == 0

    def pick(a, b):
        return tuple(jnp.where(even, i, j) for i, j in zip(a, b))

    down_a, up_a = pick(right, left), pick(left, right)
    down_b, up_b = up_a, down_a
    has_up_a = jnp.logical_or(q == 1, c > 0)
    has_down_a = jnp.logical_or(q == 0, c > 0)
    has_up_b, has_down_b = has_down_a, has_up_a
    alias_a = jnp.logical_and(first, q == 0)
    alias_b = jnp.logical_and(first, q == 1)
    is_fixed = p == 0
    fixed_peer = (p, 1 - q)

    def slot_a(k):
        return jnp.where(alias_a, B_AT + k, A_AT + k)

    def slot_b(k):
        return jnp.where(jnp.logical_and(alias_b, k >= 1), A_AT + k - 1, B_AT + k)

    def remote(src, dst, send, recv, to):
        return pltpu.make_async_remote_copy(
            src_ref=src, dst_ref=dst, send_sem=send, recv_sem=recv, device_id=to, device_id_type=MESH
        )

    def load(i):
        at = jnp.where(i == 0, A_AT, B_AT)
        which = jnp.where(i == 0, q, 1 - q)
        return pltpu.make_async_copy(factors.at[which], x.at[at, h], load_sem.at[i])

    def swap_in(i):
        at = jnp.where(i == 0, A_AT, B_AT)
        which = jnp.where(i == 0, 1 - q, q)
        return remote(factors.at[which], x.at[at, 1 - h], in_send.at[i], in_recv.at[i], partner)

    def swap_in_arrival(i):
        at = jnp.where(i == 0, A_AT, B_AT)
        return remote(factors.at[0], x.at[at, h], in_send.at[i], in_recv.at[i], partner)

    def counts_in(k):
        return pltpu.make_async_copy(counts.at[2 * k + differs], tiles.at[k], count_sem.at[k])

    def chain_a(k):
        return remote(x.at[slot_a(k), h], x.at[A_AT + k + 1, h], chain_send.at[A_AT + k], chain_recv.at[A_AT + k + 1], down_a)

    def chain_a_arrival(k):
        return remote(x.at[0, h], x.at[A_AT + k, h], chain_send.at[A_AT + k], chain_recv.at[A_AT + k], up_a)

    def chain_b(k):
        return remote(x.at[slot_b(k), h], x.at[B_AT + k + 1, h], chain_send.at[B_AT + k], chain_recv.at[B_AT + k + 1], down_b)

    def chain_b_arrival(k):
        return remote(x.at[0, h], x.at[B_AT + k, h], chain_send.at[B_AT + k], chain_recv.at[B_AT + k], up_b)

    def to_core(at):
        return remote(x.at[at, h], x.at[at, h], core_send.at[at], core_recv.at[at], sibling)

    def from_core_arrival(at):
        return remote(x.at[at, 1 - h], x.at[at, 1 - h], core_send.at[at], core_recv.at[at], sibling)

    def g_core(at):
        return remote(g.at[at, 1 - h], from_core.at[at], gcore_send.at[at], gcore_recv.at[at], sibling)

    def g_chain(at, to):
        return remote(g.at[at, h], from_chain.at[at - 1], gchain_send.at[at], gchain_recv.at[at - 1], to)

    def g_chain_arrival(at, to):
        return remote(g.at[at, h], from_chain.at[at], gchain_send.at[at], gchain_recv.at[at], to)

    def swap_out(i):
        at = jnp.where(i == 0, A_AT, B_AT)
        return remote(g.at[at, h], swapped.at[i], out_send.at[i], out_recv.at[i], partner)

    fixed_in = remote(factors.at[0], x.at[FIXED, 0], fix_send, fix_recv, fixed_peer)
    fixed_own = pltpu.make_async_copy(factors.at[0], x.at[FIXED, 1], load_sem.at[2])
    fixed_out = remote(g.at[FIXED, 1 - q], extra, gfix_send, gfix_recv, fixed_peer)
    fixed_giver = jnp.logical_and(is_fixed, q == 0)
    fixed_taker = jnp.logical_and(is_fixed, q == 1)

    @pl.when(same)
    def _():
        load(0).start()
        load(1).start()

    @pl.when(fixed_taker)
    def _():
        fixed_own.start()

    for k in range(4):
        counts_in(k).start()

    barrier = pltpu.get_barrier_semaphore()

    def greet(to):
        pl.semaphore_signal(barrier, inc=1, device_id=to, device_id_type=MESH)

    greet(sibling)
    greet(right)

    @pl.when(c > 0)
    def _():
        greet(left)

    @pl.when(other)
    def _():
        greet(partner)

    @pl.when(is_fixed)
    def _():
        greet(fixed_peer)

    greeted = 2 + jnp.where(c > 0, 1, 0) + differs + jnp.where(is_fixed, 1, 0)
    pl.semaphore_wait(barrier, greeted)

    @pl.when(other)
    def _():
        swap_in(0).start()
        swap_in(1).start()

    @pl.when(fixed_giver)
    def _():
        fixed_in.start()

    @pl.loop(0, SLOTS)
    def _(at):
        g[at] = jnp.zeros_like(g[at])

    @pl.when(fixed_taker)
    def _():
        fixed_own.wait()
        fixed_in.wait_recv()

    def relay_b(s):
        @pl.when(jnp.logical_and(has_down_b, s < 4))
        def _():
            chain_b(s).start()

        @pl.when(jnp.logical_or(has_up_b, s == 0))
        def _():
            to_core(B_AT + s).start()

    def relay_a(s):
        @pl.when(jnp.logical_and(has_down_a, s < 3))
        def _():
            chain_a(s).start()

        @pl.when(jnp.logical_or(has_up_a, s == 0))
        def _():
            to_core(A_AT + s).start()

    def meeting(k):
        a, b = slot_a(k), slot_b(k + differs)
        upper = jnp.where(is_fixed, jnp.where(even, A_AT, FIXED), jnp.where(even, a, b))
        lower = jnp.where(even, b, a)
        g_upper = jnp.where(is_fixed, FIXED, upper)
        counts_in(k).wait()
        for half in range(2):
            uh[half], ul[half] = split(x[upper, half])
            lh[half], ll[half] = split(x[lower, half])
        items = x.shape[-1]

        for start in range(0, items, tile):
            rows = pl.ds(start, tile)
            scores = 0.0
            for half in range(2):
                scores += dot3((uh[half, :, rows], ul[half, :, rows]), (lh[half], ll[half]), ((0,), (0,)))
            r = split(residual_of(scores, tiles[k, rows, :]))
            for half in range(2):
                g[lower, half] += dot3((uh[half, :, rows], ul[half, :, rows]), r, ((1,), (0,)))
                g[g_upper, half, :, rows] += dot3((lh[half], ll[half]), r, ((1,), (1,)))

    @pl.loop(0, 5)
    def _(s):
        @pl.when(s == 0)
        def _():
            @pl.when(same)
            def _():
                load(1).wait()

            @pl.when(other)
            def _():
                swap_in_arrival(1).wait_recv()

        @pl.when(jnp.logical_and(s > 0, has_up_b))
        def _():
            chain_b_arrival(s).wait_recv()

        relay_b(s)

        @pl.when(s == 0)
        def _():
            @pl.when(same)
            def _():
                load(0).wait()

            @pl.when(other)
            def _():
                swap_in_arrival(0).wait_recv()

        @pl.when(jnp.logical_and(jnp.logical_and(s > 0, s < 4), has_up_a))
        def _():
            chain_a_arrival(s).wait_recv()

        @pl.when(s < 4)
        def _():
            relay_a(s)

        @pl.when(jnp.logical_and(s == 1, other))
        def _():
            from_core_arrival(B_AT).wait_recv()

        @pl.when(s > 0)
        def _():
            k = s - 1

            @pl.when(jnp.logical_or(has_up_a, k == 0))
            def _():
                from_core_arrival(A_AT + k).wait_recv()

            @pl.when(jnp.logical_or(has_up_b, k + differs == 0))
            def _():
                from_core_arrival(B_AT + k + differs).wait_recv()

            meeting(k)

            @pl.when(s > 1)
            def _():
                g_core(A_AT + k - 1).start()
                g_core(B_AT + k - 1).start()

    @pl.when(jnp.logical_and(same, has_up_b))
    def _():
        from_core_arrival(B_AT + 4).wait_recv()

    g_core(B_AT + 4).start()
    g_core(A_AT + 3).start()
    g_core(B_AT + 3).start()

    @pl.when(is_fixed)
    def _():
        fixed_out.start()

    def send_back(at, alias, k, last, has_down, has_up, down, up):
        g_core(at).wait_recv()
        g[at, h] += from_core[at]

        @pl.when(jnp.logical_and(k < last, has_down))
        def _():
            g_chain_arrival(at, down).wait_recv()
            g[alias, h] += from_chain[at]

        @pl.when(jnp.logical_and(k > 0, has_up))
        def _():
            g_chain(at, up).start()

    @pl.loop(0, 5)
    def _(step):
        k = 4 - step

        @pl.when(k < 4)
        def _():
            send_back(A_AT + k, slot_a(k), k, 3, has_down_a, has_up_a, down_a, up_a)

        send_back(B_AT + k, slot_b(k), k, 4, has_down_b, has_up_b, down_b, up_b)

    @pl.when(other)
    def _():
        swap_out(0).start()
        swap_out(1).start()

    @pl.when(same)
    def _():
        out[q] = g[A_AT, h]
        out[1 - q] = g[B_AT, h]

    @pl.when(other)
    def _():
        swap_out(0).wait_recv()
        out[1 - q] = swapped[0]
        swap_out(1).wait_recv()
        out[q] = swapped[1]

    @pl.when(is_fixed)
    def _():
        fixed_out.wait_recv()
        out[0] += g[FIXED, q] + extra[...]

    @pl.when(other)
    def _():
        for i in range(2):
            swap_in(i).wait_send()
            swap_out(i).wait_send()

    @pl.when(fixed_giver)
    def _():
        fixed_in.wait_send()

    @pl.when(is_fixed)
    def _():
        fixed_out.wait_send()

    @pl.loop(0, 5)
    def _(k):
        @pl.when(jnp.logical_or(has_up_b, k == 0))
        def _():
            to_core(B_AT + k).wait_send()

        @pl.when(jnp.logical_and(has_down_b, k < 4))
        def _():
            chain_b(k).wait_send()

        g_core(B_AT + k).wait_send()

        @pl.when(jnp.logical_and(has_up_b, k > 0))
        def _():
            g_chain(B_AT + k, up_b).wait_send()

        @pl.when(k < 4)
        def _():
            @pl.when(jnp.logical_or(has_up_a, k == 0))
            def _():
                to_core(A_AT + k).wait_send()

            @pl.when(jnp.logical_and(has_down_a, k < 3))
            def _():
                chain_a(k).wait_send()

            g_core(A_AT + k).wait_send()

            @pl.when(jnp.logical_and(has_up_a, k > 0))
            def _():
                g_chain(A_AT + k, up_a).wait_send()


def solution(mesh):
    players = mesh.shape["blk"]
    chips = players // 2

    def body(factors, state, counts):
        share, items = factors.shape[2], factors.shape[3]
        tile = min(256, items)
        dma = pltpu.SemaphoreType.DMA
        grad = pl.pallas_call(
            functools.partial(kernel, chips, tile),
            out_shape=jax.ShapeDtypeStruct((2, share, items), F32),
            in_specs=[pl.BlockSpec(memory_space=pl.ANY)] * 2,
            out_specs=pl.BlockSpec(memory_space=pltpu.VMEM),
            scratch_shapes=[
                pltpu.VMEM((SLOTS, 2, share, items), F32),
                pltpu.VMEM((SLOTS, 2, share, items), F32),
                pltpu.VMEM((9, share, items), F32),
                pltpu.VMEM((9, share, items), F32),
                pltpu.VMEM((2, share, items), F32),
                pltpu.VMEM((share, items), F32),
                pltpu.VMEM((4, items, items), jnp.int32),
                pltpu.VMEM((2, share, items), BF16),
                pltpu.VMEM((2, share, items), BF16),
                pltpu.VMEM((2, share, items), BF16),
                pltpu.VMEM((2, share, items), BF16),
                dma((3,)), dma((4,)),
                dma((2,)), dma((2,)), dma, dma,
                dma((9,)), dma((9,)), dma((9,)), dma((9,)),
                dma((9,)), dma((9,)), dma((9,)), dma((9,)),
                dma((2,)), dma((2,)), dma, dma,
            ],
            compiler_params=pltpu.CompilerParams(
                collective_id=0, has_side_effects=True, vmem_limit_bytes=60 * 1024 * 1024
            ),
        )(factors[0], counts[0])
        grad = grad[None]
        new_state = state + grad * grad
        step = grad / jnp.sqrt(new_state)
        return (step, new_state)

    in_specs = (
        P("blk", None, "rep", None),
        P("blk", None, "rep", None),
        P("blk", None, None, None),
    )
    out_specs = (P("blk", None, "rep", None), P("blk", None, "rep", None))
    return jax.shard_map(body, mesh=mesh, in_specs=in_specs, out_specs=out_specs, check_vma=False)
```

time: 339 us -> 111 us (0.33)
  the two profiles are of different devices: /device:TPU:2 before, /device:TPU:195 now
where the time goes in v1:
time: 111 us
  Pallas kernels  104 us (94%)
  local copies, waits for them, and re-layouts  4.68 us (4%)
  other arithmetic  1.27 us (1%)
    pallas_call x1, Pallas kernels, body(): pl.pallas_call(functools.partial(kernel, chips, tile), out_shape=jax.Shap...  104 us
    unnamed x5, local copies, waits for them, and re-layouts  4.68 us

profile of v1, /device:TPU:195, one launch (start us, length us, event | category | flops | bytes accessed | tf_op | source)
XLA Modules:
  0.0 110.7 jit_solution(14994035755140479493)
XLA Ops:
  0.6 0.0 copy-start
  0.6 2.1 %copy.13 = f32[1,2,150,512]{3,2,1,0:T(8,128)} copy(f32[1,2,150,512]{3,1,2,0:T(2,128)} %param.3) | data formatting | bytes 1228800 | tf_op args[0]
  2.7 104.1 %shard_map.50 = f32[2,150,512]{2,1,0:T(8,128)} custom-call(f32[2,150,512]{2,1,0:T(8,128)} %bitcast.11, s32[8,512,512]{2,1,0:T(8,128)} %bitcast.10), custom_call_target="tpu_custom_call" | custom-call | tf_op jit(solution)/shard_map/pallas_call | solution.py:404
  106.8 0.0 copy-done
  106.8 1.3 %bitcast_add_fusion = (f32[1,2,150,512]{3,2,1,0:T(8,128)S(1)}, f32[1,2,150,512]{3,2,1,0:T(8,128)S(1)}) fusion(f32[1,2,150,512]{3,1,2,0:T(2,128)S(1)} %copy-done, f32[2,150,512]{2,1,0:T(8,128)} %shard_map.50), kind=kLoop, calls=%fused_computation | loop fusion | flops 460800 | bytes 2457600 | tf_op jit(solution)/shard_map/add | solution.py:432
  108.1 1.3 %copy.8 = f32[1,2,150,512]{3,1,2,0:T(2,128)} copy(f32[1,2,150,512]{3,2,1,0:T(8,128)S(1)} %get-tuple-element.4) | data formatting | bytes 1228800
  109.4 1.3 %copy.7 = f32[1,2,150,512]{3,1,2,0:T(2,128)} copy(f32[1,2,150,512]{3,2,1,0:T(8,128)S(1)} %get-tuple-element.5) | data formatting | bytes 1228800
Async XLA Ops:
  0.6 106.2 %copy-start = (f32[1,2,150,512]{3,1,2,0:T(2,128)S(1)}, f32[1,2,150,512]{3,1,2,0:T(2,128)}, u32[]{:S(2)}) copy-start(f32[1,2,150,512]{3,1,2,0:T(2,128)} %param.4) | copy-start | bytes 1843204

commit v2 on v1

v2 whole, which is shorter than its diff:
```python
import functools

import jax
import jax.numpy as jnp
from jax import lax
from jax.experimental import pallas as pl
from jax.experimental.pallas import tpu as pltpu
from jax.sharding import PartitionSpec as P

MESH = pl.DeviceIdType.MESH
BF16 = jnp.bfloat16
F32 = jnp.float32
clip_bound = 2.0

A_AT, B_AT, FIXED, SLOTS = 0, 4, 9, 10


def residual_of(scores, count_tile):
    amount = count_tile.astype(F32)
    present = count_tile > 0
    clamped = jnp.maximum(amount, 1.0)
    weight = 0.1 + 0.25 * jnp.sqrt(clamped)
    kept = weight * jnp.clip(scores - jnp.log(clamped), -clip_bound, clip_bound)
    return jnp.where(present, kept, 0.5 * jax.nn.sigmoid(scores))


def split(value):
    high = value.astype(BF16)
    return high, (value - high.astype(F32)).astype(BF16)


def dot3(left, right, dims):
    (lh, ll), (rh, rl) = left, right

    def one(a, b):
        return lax.dot_general(a, b, (dims, ((), ())), preferred_element_type=F32)

    return one(lh, rh) + one(lh, rl) + one(ll, rh)


def kernel(
    chips, tile, factors, counts, out,
    x, g, from_core, from_chain, returned, swapped, extra, tiles, uh, ul, lh, ll,
    load_sem, count_sem,
    in_send, in_recv, fix_send, fix_recv,
    out_block_send, block_recv, core_send, core_recv,
    gcore_send, gcore_recv, gback_send, gchain_recv, returned_recv,
    out_send, out_recv, gfix_send, gfix_recv,
):
    p, q = lax.axis_index("blk"), lax.axis_index("rep")
    c, h = p // 2, p % 2
    differs = (h + q) % 2
    same = differs == 0
    other = differs == 1
    even, odd = q == 0, q == 1

    def both(*conditions):
        return functools.reduce(jnp.logical_and, conditions)

    def either(*conditions):
        return functools.reduce(jnp.logical_or, conditions)

    def pick(condition, a, b):
        return tuple(jnp.where(condition, i, j) for i, j in zip(a, b))

    def ahead(n):
        over = c + n >= chips
        return (jnp.where(over, 2 * chips - 1 - c - n, c + n) * 2 + h, jnp.where(over, 1 - q, q))

    def at_chip(chip):
        return (jnp.maximum(chip, 0) * 2 + h, q)

    sibling = (c * 2 + 1 - h, q)
    partner = (c * 2 + 1 - h, 1 - q)
    fixed_peer = (p, 1 - q)
    right, left = ahead(1), at_chip(c - 1)
    down_a, up_a = pick(even, right, left), pick(even, left, right)
    down_b, up_b = up_a, down_a
    has_up_a = either(odd, c > 0)
    has_down_a = either(even, c > 0)
    has_up_b, has_down_b = has_down_a, has_up_a
    alias_a, alias_b = both(even, c == 0), both(odd, c == 0)
    is_fixed = p == 0

    has_b3, has_b4 = either(even, c >= 2), either(even, c >= 1)
    far = (
        (either(even, c >= 3, c == 0), pick(even, ahead(3), at_chip(jnp.where(c == 0, 2, c - 3))),
         jnp.where(alias_a, B_AT, A_AT), jnp.where(alias_b, B_AT + 3, A_AT + 3)),
        (either(odd, c >= 1), pick(odd, ahead(3), at_chip(jnp.where(c >= 3, c - 3, 3 - c))),
         B_AT, jnp.where(both(even, c < 3), A_AT + 3, B_AT + 3)),
        (either(odd, c >= 4), pick(odd, ahead(4), at_chip(c - 4)), B_AT, B_AT + 4),
        (both(odd, c <= 2), at_chip(3 - c), A_AT, B_AT + 4),
    )
    from_a3 = (has_up_a, pick(even, at_chip(jnp.where(c >= 3, c - 3, 3 - c)), ahead(3)),
               jnp.where(both(even, c < 3), 1, 0))
    from_b3 = (has_b3, pick(even, ahead(3), at_chip(jnp.where(c >= 3, c - 3, 2 - c))),
               jnp.where(both(odd, c == 2), 0, 1))
    from_b4 = (has_b4, pick(even, ahead(4), at_chip(jnp.where(c >= 4, c - 4, 3 - c))),
               jnp.where(both(odd, c < 4), 3, 2))

    def slot_a(k):
        return jnp.where(alias_a, B_AT + k, A_AT + k)

    def slot_b(k):
        at = jnp.where(both(alias_b, k >= 1), A_AT + k - 1, B_AT + k)
        return jnp.where(both(odd, c == 1, k == 3), A_AT, at)

    def remote(src, dst, send, recv, to):
        return pltpu.make_async_remote_copy(
            src_ref=src, dst_ref=dst, send_sem=send, recv_sem=recv, device_id=to, device_id_type=MESH
        )

    def load(i):
        at = jnp.where(i == 0, A_AT, B_AT)
        which = jnp.where(i == 0, q, 1 - q)
        return pltpu.make_async_copy(factors.at[which], x.at[at, h], load_sem.at[i])

    def swap_in(i):
        at = jnp.where(i == 0, A_AT, B_AT)
        which = jnp.where(i == 0, 1 - q, q)
        return remote(factors.at[which], x.at[at, 1 - h], in_send.at[i], in_recv.at[i], partner)

    def swap_in_arrival(i):
        at = jnp.where(i == 0, A_AT, B_AT)
        return remote(factors.at[0], x.at[at, h], in_send.at[i], in_recv.at[i], partner)

    def counts_in(k):
        return pltpu.make_async_copy(counts.at[2 * k + differs], tiles.at[k], count_sem.at[k])

    def chain_a(k):
        to = A_AT + k + 1
        return remote(x.at[slot_a(k), h], x.at[to, h], out_block_send.at[4 + k], block_recv.at[to], down_a)

    def chain_b(k):
        to = B_AT + k + 1
        return remote(x.at[slot_b(k), h], x.at[to, h], out_block_send.at[6 + k], block_recv.at[to], down_b)

    def far_block(i):
        _, to, at, into = far[i]
        return remote(x.at[at, h], x.at[into, h], out_block_send.at[i], block_recv.at[into], to)

    def arrival(at):
        return remote(x.at[at, h], x.at[at, h], out_block_send.at[0], block_recv.at[at], sibling)

    def to_core(at):
        return remote(x.at[at, h], x.at[at, h], core_send.at[at], core_recv.at[at], sibling)

    def from_core_arrival(at):
        return remote(x.at[at, 1 - h], x.at[at, 1 - h], core_send.at[at], core_recv.at[at], sibling)

    def g_core(at):
        return remote(g.at[at, 1 - h], from_core.at[at], gcore_send.at[at], gcore_recv.at[at], sibling)

    def g_chain(at, to):
        return remote(g.at[at, h], from_chain.at[at - 1], gback_send.at[at], gchain_recv.at[at - 1], to)

    def g_chain_arrival(at):
        return remote(g.at[at, h], from_chain.at[at], gback_send.at[at], gchain_recv.at[at], sibling)

    def g_return(at, source):
        _, to, i = source
        return remote(g.at[at, h], returned.at[i], gback_send.at[at], returned_recv.at[i], to)

    def g_return_arrival(i):
        return remote(g.at[0, h], returned.at[i], gback_send.at[0], returned_recv.at[i], sibling)

    def swap_out(i):
        at = jnp.where(i == 0, A_AT, B_AT)
        return remote(g.at[at, h], swapped.at[i], out_send.at[i], out_recv.at[i], partner)

    fixed_in = remote(factors.at[0], x.at[FIXED, 0], fix_send, fix_recv, fixed_peer)
    fixed_own = pltpu.make_async_copy(factors.at[0], x.at[FIXED, 1], load_sem.at[2])
    fixed_out = remote(g.at[FIXED, 1 - q], extra, gfix_send, gfix_recv, fixed_peer)
    fixed_giver = both(is_fixed, even)
    fixed_taker = both(is_fixed, odd)

    def when(condition, action):
        @pl.when(condition)
        def _():
            action()

    @pl.when(same)
    def _():
        load(0).start()
        load(1).start()

    when(fixed_taker, fixed_own.start)
    for k in range(4):
        counts_in(k).start()

    barrier = pltpu.get_barrier_semaphore()
    peers = [
        (None, sibling), (None, right), (c > 0, left), (other, partner), (is_fixed, fixed_peer),
        *[(f[0], f[1]) for f in far], from_a3[:2], from_b3[:2], from_b4[:2],
    ]
    greeted = 0
    for condition, to in peers:
        def greet(to=to):
            pl.semaphore_signal(barrier, inc=1, device_id=to, device_id_type=MESH)

        if condition is None:
            greet()
            greeted += 1
        else:
            when(condition, greet)
            greeted += jnp.where(condition, 1, 0)
    pl.semaphore_wait(barrier, greeted)

    @pl.when(other)
    def _():
        swap_in(1).start()
        swap_in(0).start()

    when(fixed_giver, fixed_in.start)

    @pl.loop(0, SLOTS)
    def _(at):
        g[at] = jnp.zeros_like(g[at])

    for i, stream, has_down in ((1, chain_b, has_down_b), (0, chain_a, has_down_a)):
        when(same, load(i).wait)
        when(other, swap_in_arrival(i).wait_recv)
        when(has_down, stream(0).start)
        to_core(A_AT if i == 0 else B_AT).start()
    for i in (1, 0, 2, 3):
        when(far[i][0], far_block(i).start)

    @pl.when(fixed_taker)
    def _():
        fixed_own.wait()
        fixed_in.wait_recv()

    def meeting(k):
        a, b = slot_a(k), slot_b(k + differs)
        upper = jnp.where(is_fixed, jnp.where(even, A_AT, FIXED), jnp.where(even, a, b))
        lower = jnp.where(even, b, a)
        g_upper = jnp.where(is_fixed, FIXED, upper)
        counts_in(k).wait()
        for half in range(2):
            uh[half], ul[half] = split(x[upper, half])
            lh[half], ll[half] = split(x[lower, half])
        items = x.shape[-1]

        for start in range(0, items, tile):
            rows = pl.ds(start, tile)
            scores = 0.0
            for half in range(2):
                scores += dot3((uh[half, :, rows], ul[half, :, rows]), (lh[half], ll[half]), ((0,), (0,)))
            r = split(residual_of(scores, tiles[k, rows, :]))
            for half in range(2):
                g[lower, half] += dot3((uh[half, :, rows], ul[half, :, rows]), r, ((1,), (0,)))
                g[g_upper, half, :, rows] += dot3((lh[half], ll[half]), r, ((1,), (1,)))

    has = {1: has_up_a, 2: has_up_a, 3: has_up_a, 5: has_up_b, 6: has_up_b, 7: has_b3, 8: has_b4}

    def pass_on(at, stream=None, has_down=None):
        when(has[at], arrival(at).wait_recv)
        if stream is not None:
            when(has_down, stream(1).start)
        when(has[at], to_core(at).start)

    def other_half(at, condition=None):
        conditions = [i for i in (has.get(at), condition) if i is not None]
        if conditions:
            when(both(*conditions), from_core_arrival(at).wait_recv)
        else:
            from_core_arrival(at).wait_recv()

    def gathered(at):
        g_core(at).wait_recv()
        g[at, h] += from_core[at]

    def give_back(at, source):
        gathered(at)
        when(source[0], g_return(at, source).start)

    order = (0, jnp.where(same, 1, 3), jnp.where(same, 3, 2), jnp.where(same, 2, 1))

    @pl.loop(0, 4)
    def _(turn):
        @pl.when(turn == 0)
        def _():
            pass_on(B_AT + 1, chain_b, has_down_b)
            pass_on(A_AT + 1, chain_a, has_down_a)
            other_half(B_AT)
            other_half(A_AT)
            other_half(B_AT + 1, other)

        @pl.when(turn == 1)
        def _():
            pass_on(B_AT + 4)
            pass_on(B_AT + 3)
            pass_on(A_AT + 3)
            other_half(A_AT + 1, same)
            other_half(B_AT + 1, same)
            other_half(A_AT + 3, other)
            other_half(B_AT + 3, other)
            other_half(B_AT + 4, other)

        @pl.when(turn == 2)
        def _():
            g_core(B_AT + 4).start()
            pass_on(B_AT + 2)
            pass_on(A_AT + 2)
            other_half(A_AT + 3, same)
            other_half(B_AT + 3, same)
            other_half(A_AT + 2, either(other, alias_b))
            other_half(B_AT + 2, other)

        @pl.when(turn == 3)
        def _():
            g_core(A_AT + 3).start()
            g_core(B_AT + 3).start()
            give_back(B_AT + 4, from_b4)
            give_back(A_AT + 3, from_a3)
            give_back(B_AT + 3, from_b3)
            other_half(A_AT + 1, other)
            other_half(A_AT + 2, both(same, jnp.logical_not(alias_b)))
            other_half(B_AT + 2, same)

        k = jnp.where(turn == 0, order[0], jnp.where(turn == 1, order[1], jnp.where(turn == 2, order[2], order[3])))
        meeting(k)

    for k in (2, 1, 0):
        g_core(A_AT + k).start()
        g_core(B_AT + k).start()
    when(is_fixed, fixed_out.start)

    def chained(at, alias, has_down):
        @pl.when(has_down)
        def _():
            g_chain_arrival(at).wait_recv()
            g[alias, h] += from_chain[at]

    def add_returned(i, at):
        @pl.when(far[i][0])
        def _():
            g_return_arrival(i).wait_recv()
            g[at, h] += returned[i]

    gathered(A_AT + 2)
    when(has_up_a, g_chain(A_AT + 2, up_a).start)
    gathered(B_AT + 2)
    when(has_up_b, g_chain(B_AT + 2, up_b).start)
    gathered(A_AT + 1)
    gathered(B_AT + 1)
    chained(A_AT + 1, slot_a(1), has_down_a)
    when(has_up_a, g_chain(A_AT + 1, up_a).start)
    chained(B_AT + 1, slot_b(1), has_down_b)
    when(has_up_b, g_chain(B_AT + 1, up_b).start)
    gathered(A_AT)
    gathered(B_AT)
    for i in (0, 1, 2, 3):
        add_returned(i, far[i][2])
    chained(A_AT, slot_a(0), has_down_a)

    @pl.when(other)
    def _():
        swap_out(0).start()

    @pl.when(same)
    def _():
        out[q] = g[A_AT, h]

    chained(B_AT, B_AT, has_down_b)

    @pl.when(other)
    def _():
        swap_out(1).start()
        swap_out(0).wait_recv()
        out[1 - q] = swapped[0]
        swap_out(1).wait_recv()
        out[q] = swapped[1]

    @pl.when(same)
    def _():
        out[1 - q] = g[B_AT, h]

    @pl.when(is_fixed)
    def _():
        fixed_out.wait_recv()
        out[0] += g[FIXED, q] + extra[...]

    other_half(B_AT + 4, same)

    @pl.when(other)
    def _():
        for i in range(2):
            swap_in(i).wait_send()
            swap_out(i).wait_send()

    when(fixed_giver, fixed_in.wait_send)
    when(is_fixed, fixed_out.wait_send)
    for i in range(4):
        when(far[i][0], far_block(i).wait_send)
    for k in range(2):
        when(has_down_a, chain_a(k).wait_send)
        when(has_down_b, chain_b(k).wait_send)
    for at in range(9):
        if at in has:
            when(has[at], to_core(at).wait_send)
        else:
            to_core(at).wait_send()
        g_core(at).wait_send()
    for k in (1, 2):
        when(has_up_a, g_chain(A_AT + k, up_a).wait_send)
        when(has_up_b, g_chain(B_AT + k, up_b).wait_send)
    when(from_a3[0], g_return(A_AT + 3, from_a3).wait_send)
    when(from_b3[0], g_return(B_AT + 3, from_b3).wait_send)
    when(from_b4[0], g_return(B_AT + 4, from_b4).wait_send)


def solution(mesh):
    players = mesh.shape["blk"]
    chips = players // 2

    def body(factors, state, counts):
        share, items = factors.shape[2], factors.shape[3]
        tile = min(512, items)
        dma = pltpu.SemaphoreType.DMA
        grad = pl.pallas_call(
            functools.partial(kernel, chips, tile),
            out_shape=jax.ShapeDtypeStruct((2, share, items), F32),
            in_specs=[pl.BlockSpec(memory_space=pl.ANY)] * 2,
            out_specs=pl.BlockSpec(memory_space=pltpu.VMEM),
            scratch_shapes=[
                pltpu.VMEM((SLOTS, 2, share, items), F32),
                pltpu.VMEM((SLOTS, 2, share, items), F32),
                pltpu.VMEM((9, share, items), F32),
                pltpu.VMEM((6, share, items), F32),
                pltpu.VMEM((4, share, items), F32),
                pltpu.VMEM((2, share, items), F32),
                pltpu.VMEM((share, items), F32),
                pltpu.VMEM((4, items, items), jnp.int32),
                pltpu.VMEM((2, share, items), BF16),
                pltpu.VMEM((2, share, items), BF16),
                pltpu.VMEM((2, share, items), BF16),
                pltpu.VMEM((2, share, items), BF16),
                dma((3,)), dma((4,)),
                dma((2,)), dma((2,)), dma, dma,
                dma((8,)), dma((9,)), dma((9,)), dma((9,)),
                dma((9,)), dma((9,)), dma((9,)), dma((6,)), dma((4,)),
                dma((2,)), dma((2,)), dma, dma,
            ],
            compiler_params=pltpu.CompilerParams(
                collective_id=0, has_side_effects=True, vmem_limit_bytes=60 * 1024 * 1024
            ),
        )(factors[0], counts[0])
        grad = grad[None]
        new_state = state + grad * grad
        step = grad / jnp.sqrt(new_state)
        return (step, new_state)

    in_specs = (
        P("blk", None, "rep", None),
        P("blk", None, "rep", None),
        P("blk", None, None, None),
    )
    out_specs = (P("blk", None, "rep", None), P("blk", None, "rep", None))
    return jax.shard_map(body, mesh=mesh, in_specs=in_specs, out_specs=out_specs, check_vma=False)
```

time: 111 us -> 122 us (1.099)
  the two profiles are of different devices: /device:TPU:195 before, /device:TPU:243 now
where the time goes in v2:
time: 122 us; the launch traced here: 120 us
  Pallas kernels  114 us (93%)
  local copies, waits for them, and re-layouts  4.68 us (4%)
  other arithmetic  1.27 us (1%)
    pallas_call x1, Pallas kernels, body(): pl.pallas_call(functools.partial(kernel, chips, tile), out_shape=jax.Shap...  114 us
    unnamed x5, local copies, waits for them, and re-layouts  4.68 us

profile of v2, /device:TPU:243, one launch (start us, length us, event | category | flops | bytes accessed | tf_op | source)
XLA Modules:
  0.0 120.1 jit_solution(9066583348224140587)
XLA Ops:
  0.6 0.0 copy-start
  0.6 2.1 %copy.13 = f32[1,2,150,512]{3,2,1,0:T(8,128)} copy(f32[1,2,150,512]{3,1,2,0:T(2,128)} %param.3) | data formatting | bytes 1228800 | tf_op args[0]
  2.7 113.5 %shard_map.50 = f32[2,150,512]{2,1,0:T(8,128)} custom-call(f32[2,150,512]{2,1,0:T(8,128)} %bitcast.11, s32[8,512,512]{2,1,0:T(8,128)} %bitcast.10), custom_call_target="tpu_custom_call" | custom-call | tf_op jit(solution)/shard_map/pallas_call | solution.py:421
  116.2 0.0 copy-done
  116.3 1.3 %bitcast_add_fusion = (f32[1,2,150,512]{3,2,1,0:T(8,128)S(1)}, f32[1,2,150,512]{3,2,1,0:T(8,128)S(1)}) fusion(f32[1,2,150,512]{3,1,2,0:T(2,128)S(1)} %copy-done, f32[2,150,512]{2,1,0:T(8,128)} %shard_map.50), kind=kLoop, calls=%fused_computation | loop fusion | flops 460800 | bytes 2457600 | tf_op jit(solution)/shard_map/add | solution.py:450
  117.5 1.3 %copy.8 = f32[1,2,150,512]{3,1,2,0:T(2,128)} copy(f32[1,2,150,512]{3,2,1,0:T(8,128)S(1)} %get-tuple-element.4) | data formatting | bytes 1228800
  118.8 1.3 %copy.7 = f32[1,2,150,512]{3,1,2,0:T(2,128)} copy(f32[1,2,150,512]{3,2,1,0:T(8,128)S(1)} %get-tuple-element.5) | data formatting | bytes 1228800
Async XLA Ops:
  0.6 115.6 %copy-start = (f32[1,2,150,512]{3,1,2,0:T(2,128)S(1)}, f32[1,2,150,512]{3,1,2,0:T(2,128)}, u32[]{:S(2)}) copy-start(f32[1,2,150,512]{3,1,2,0:T(2,128)} %param.4) | copy-start | bytes 1843204

commit v3 on v2

--- a/solution.py
+++ b/solution.py
@@ -13,6 +13,7 @@
 clip_bound = 2.0
 
 A_AT, B_AT, FIXED, SLOTS = 0, 4, 9, 10
+LANES = 128
 
 
 def residual_of(scores, count_tile):
@@ -38,9 +39,19 @@
     return one(lh, rh) + one(lh, rl) + one(ll, rh)
 
 
+def pack(blocks):
+    two, share, items = blocks.shape
+    return blocks.reshape(two, share, items // LANES, LANES).transpose(1, 2, 0, 3).reshape(-1, LANES)
+
+
+def unpack(rows, dims):
+    one, two, share, items = dims
+    return rows.reshape(share, items // LANES, two, LANES).transpose(2, 0, 1, 3).reshape(dims)
+
+
 def kernel(
     chips, tile, factors, counts, out,
-    x, g, from_core, from_chain, returned, swapped, extra, tiles, uh, ul, lh, ll,
+    x, g, raw, mine, from_core, from_chain, returned, swapped, extra, tiles, uh, ul, lh, ll,
     load_sem, count_sem,
     in_send, in_recv, fix_send, fix_recv,
     out_block_send, block_recv, core_send, core_recv,
@@ -82,20 +93,55 @@
     alias_a, alias_b = both(even, c == 0), both(odd, c == 0)
     is_fixed = p == 0
 
+    half_way = chips // 2
+
+    def right_fed(chip):
+        return both(chip >= half_way, chip < half_way + 3)
+
+    def left_fed(chip):
+        return either(both(chip >= half_way - 3, chip < half_way), chip >= chips - 3)
+
+    def fed_a3(to):
+        return jnp.where(to[1] == 0, right_fed(to[0] // 2), left_fed(to[0] // 2))
+
+    def fed_b3(to):
+        return jnp.where(to[1] == 0, left_fed(to[0] // 2), right_fed(to[0] // 2))
+
+    def fed_b4(to):
+        return both(to[1] == 0, to[0] // 2 == chips - 4)
+
+    here = (p, q)
+    near = either(both(c >= half_way - 3, c < half_way + 3), c >= chips - 4)
+    plain = jnp.logical_not(near)
+    send_a2, send_b2 = both(has_down_a, fed_a3(down_a)), both(has_down_b, fed_b3(down_b))
+    send_b3 = both(has_down_b, fed_b4(down_b))
+
     has_b3, has_b4 = either(even, c >= 2), either(even, c >= 1)
+    far_to = (
+        pick(even, ahead(3), at_chip(jnp.where(c == 0, 2, c - 3))),
+        pick(odd, ahead(3), at_chip(jnp.where(c >= 3, c - 3, 3 - c))),
+        pick(odd, ahead(4), at_chip(c - 4)),
+        at_chip(3 - c),
+    )
+    first_to_b, second_to_a = alias_b, both(even, c < 3)
+    not_fed = (
+        jnp.logical_not(jnp.where(first_to_b, fed_b3(far_to[0]), fed_a3(far_to[0]))),
+        jnp.logical_not(jnp.where(second_to_a, fed_a3(far_to[1]), fed_b3(far_to[1]))),
+        jnp.logical_not(fed_b4(far_to[2])),
+    )
     far = (
-        (either(even, c >= 3, c == 0), pick(even, ahead(3), at_chip(jnp.where(c == 0, 2, c - 3))),
-         jnp.where(alias_a, B_AT, A_AT), jnp.where(alias_b, B_AT + 3, A_AT + 3)),
-        (either(odd, c >= 1), pick(odd, ahead(3), at_chip(jnp.where(c >= 3, c - 3, 3 - c))),
-         B_AT, jnp.where(both(even, c < 3), A_AT + 3, B_AT + 3)),
-        (either(odd, c >= 4), pick(odd, ahead(4), at_chip(c - 4)), B_AT, B_AT + 4),
-        (both(odd, c <= 2), at_chip(3 - c), A_AT, B_AT + 4),
+        (both(either(even, c >= 3, c == 0), not_fed[0]), far_to[0],
+         jnp.where(alias_a, B_AT, A_AT), jnp.where(first_to_b, B_AT + 3, A_AT + 3)),
+        (both(either(odd, c >= 1), not_fed[1]), far_to[1],
+         B_AT, jnp.where(second_to_a, A_AT + 3, B_AT + 3)),
+        (both(either(odd, c >= 4), not_fed[2]), far_to[2], B_AT, B_AT + 4),
+        (both(odd, c <= 2), far_to[3], A_AT, B_AT + 4),
     )
-    from_a3 = (has_up_a, pick(even, at_chip(jnp.where(c >= 3, c - 3, 3 - c)), ahead(3)),
+    from_a3 = (both(has_up_a, jnp.logical_not(fed_a3(here))), pick(even, at_chip(jnp.where(c >= 3, c - 3, 3 - c)), ahead(3)),
                jnp.where(both(even, c < 3), 1, 0))
-    from_b3 = (has_b3, pick(even, ahead(3), at_chip(jnp.where(c >= 3, c - 3, 2 - c))),
+    from_b3 = (both(has_b3, jnp.logical_not(fed_b3(here))), pick(even, ahead(3), at_chip(jnp.where(c >= 3, c - 3, 2 - c))),
                jnp.where(both(odd, c == 2), 0, 1))
-    from_b4 = (has_b4, pick(even, ahead(4), at_chip(jnp.where(c >= 4, c - 4, 3 - c))),
+    from_b4 = (both(has_b4, jnp.logical_not(fed_b4(here))), pick(even, ahead(4), at_chip(jnp.where(c >= 4, c - 4, 3 - c))),
                jnp.where(both(odd, c < 4), 3, 2))
 
     def slot_a(k):
@@ -110,19 +156,8 @@
             src_ref=src, dst_ref=dst, send_sem=send, recv_sem=recv, device_id=to, device_id_type=MESH
         )
 
-    def load(i):
-        at = jnp.where(i == 0, A_AT, B_AT)
-        which = jnp.where(i == 0, q, 1 - q)
-        return pltpu.make_async_copy(factors.at[which], x.at[at, h], load_sem.at[i])
-
-    def swap_in(i):
-        at = jnp.where(i == 0, A_AT, B_AT)
-        which = jnp.where(i == 0, 1 - q, q)
-        return remote(factors.at[which], x.at[at, 1 - h], in_send.at[i], in_recv.at[i], partner)
-
-    def swap_in_arrival(i):
-        at = jnp.where(i == 0, A_AT, B_AT)
-        return remote(factors.at[0], x.at[at, h], in_send.at[i], in_recv.at[i], partner)
+    own = pltpu.make_async_copy(factors, mine, load_sem.at[0])
+    swap_in = remote(factors, raw, in_send, in_recv, partner)
 
     def counts_in(k):
         return pltpu.make_async_copy(counts.at[2 * k + differs], tiles.at[k], count_sem.at[k])
@@ -133,7 +168,7 @@
 
     def chain_b(k):
         to = B_AT + k + 1
-        return remote(x.at[slot_b(k), h], x.at[to, h], out_block_send.at[6 + k], block_recv.at[to], down_b)
+        return remote(x.at[slot_b(k), h], x.at[to, h], out_block_send.at[7 + k], block_recv.at[to], down_b)
 
     def far_block(i):
         _, to, at, into = far[i]
@@ -168,8 +203,7 @@
         at = jnp.where(i == 0, A_AT, B_AT)
         return remote(g.at[at, h], swapped.at[i], out_send.at[i], out_recv.at[i], partner)
 
-    fixed_in = remote(factors.at[0], x.at[FIXED, 0], fix_send, fix_recv, fixed_peer)
-    fixed_own = pltpu.make_async_copy(factors.at[0], x.at[FIXED, 1], load_sem.at[2])
+    fixed_in = remote(x.at[A_AT, 0], x.at[FIXED, 0], fix_send, fix_recv, fixed_peer)
     fixed_out = remote(g.at[FIXED, 1 - q], extra, gfix_send, gfix_recv, fixed_peer)
     fixed_giver = both(is_fixed, even)
     fixed_taker = both(is_fixed, odd)
@@ -179,12 +213,21 @@
         def _():
             action()
 
-    @pl.when(same)
-    def _():
-        load(0).start()
-        load(1).start()
-
-    when(fixed_taker, fixed_own.start)
+    share, items = x.shape[2], x.shape[3]
+    groups = items // LANES
+
+    def rows_of(block, group):
+        return pl.ds(2 * group + block, share, stride=2 * groups)
+
+    def take(source, block, at, half):
+        for group in range(groups):
+            x[at, half, :, pl.ds(group * LANES, LANES)] = source[rows_of(block, group), :]
+
+    def give(block, value):
+        for group in range(groups):
+            out[rows_of(block, group), :] = value[:, group * LANES : (group + 1) * LANES]
+
+    when(either(same, fixed_taker), own.start)
     for k in range(4):
         counts_in(k).start()
 
@@ -206,28 +249,32 @@
             greeted += jnp.where(condition, 1, 0)
     pl.semaphore_wait(barrier, greeted)
 
-    @pl.when(other)
-    def _():
-        swap_in(1).start()
-        swap_in(0).start()
-
-    when(fixed_giver, fixed_in.start)
+    when(other, swap_in.start)
 
     @pl.loop(0, SLOTS)
     def _(at):
         g[at] = jnp.zeros_like(g[at])
 
-    for i, stream, has_down in ((1, chain_b, has_down_b), (0, chain_a, has_down_a)):
-        when(same, load(i).wait)
-        when(other, swap_in_arrival(i).wait_recv)
-        when(has_down, stream(0).start)
-        to_core(A_AT if i == 0 else B_AT).start()
+    when(either(same, fixed_taker), own.wait)
+    for source, condition in ((mine, same), (raw, other)):
+        @pl.when(condition)
+        def _(source=source):
+            if source is raw:
+                swap_in.wait_recv()
+            for block in range(2):
+                take(source, block, jnp.where(q == block, A_AT, B_AT), h)
+
+    when(has_down_b, chain_b(0).start)
+    when(has_down_a, chain_a(0).start)
+    to_core(B_AT).start()
+    to_core(A_AT).start()
     for i in (1, 0, 2, 3):
         when(far[i][0], far_block(i).start)
+    when(fixed_giver, fixed_in.start)
 
     @pl.when(fixed_taker)
     def _():
-        fixed_own.wait()
+        take(mine, 0, FIXED, 1)
         fixed_in.wait_recv()
 
     def meeting(k):
@@ -239,7 +286,6 @@
         for half in range(2):
             uh[half], ul[half] = split(x[upper, half])
             lh[half], ll[half] = split(x[lower, half])
-        items = x.shape[-1]
 
         for start in range(0, items, tile):
             rows = pl.ds(start, tile)
@@ -253,11 +299,20 @@
 
     has = {1: has_up_a, 2: has_up_a, 3: has_up_a, 5: has_up_b, 6: has_up_b, 7: has_b3, 8: has_b4}
 
-    def pass_on(at, stream=None, has_down=None):
+    def pass_on(at, copy=None, condition=None):
         when(has[at], arrival(at).wait_recv)
-        if stream is not None:
-            when(has_down, stream(1).start)
+        if copy is not None:
+            when(condition, copy.start)
         when(has[at], to_core(at).start)
+
+    def second_blocks():
+        pass_on(B_AT + 2, chain_b(2), send_b2)
+        pass_on(A_AT + 2, chain_a(2), send_a2)
+
+    def far_blocks():
+        pass_on(B_AT + 3, chain_b(3), send_b3)
+        pass_on(A_AT + 3)
+        pass_on(B_AT + 4)
 
     def other_half(at, condition=None):
         conditions = [i for i in (has.get(at), condition) if i is not None]
@@ -270,57 +325,88 @@
         g_core(at).wait_recv()
         g[at, h] += from_core[at]
 
-    def give_back(at, source):
-        gathered(at)
+    def give_back(at, source, present, up):
         when(source[0], g_return(at, source).start)
-
-    order = (0, jnp.where(same, 1, 3), jnp.where(same, 3, 2), jnp.where(same, 2, 1))
+        when(both(present, jnp.logical_not(source[0])), g_chain(at, up).start)
+
+    def far_back():
+        g_core(B_AT + 4).start()
+        g_core(A_AT + 3).start()
+        g_core(B_AT + 3).start()
+        gathered(B_AT + 4)
+        give_back(B_AT + 4, from_b4, has_b4, up_b)
+        gathered(A_AT + 3)
+        give_back(A_AT + 3, from_a3, has_up_a, up_a)
+        gathered(B_AT + 3)
+
+        @pl.when(send_b3)
+        def _():
+            g_chain_arrival(B_AT + 3).wait_recv()
+            g[B_AT + 3, h] += from_chain[B_AT + 3]
+
+        give_back(B_AT + 3, from_b3, has_b3, up_b)
+
+    def in_turn(*ks):
+        turn_at = ks[-1]
+        for i in range(len(ks) - 2, -1, -1):
+            turn_at = jnp.where(turn_now[0] == i, ks[i], turn_at)
+        return turn_at
+
+    near_same, near_other = both(near, same), both(near, other)
+    plain_same, plain_other = both(plain, same), both(plain, other)
+    turn_now = [0]
+    order = (
+        0,
+        jnp.where(plain_other, 3, 1),
+        jnp.where(plain_same, 3, 2),
+        jnp.where(near, 3, jnp.where(same, 2, 1)),
+    )
 
     @pl.loop(0, 4)
     def _(turn):
+        turn_now[0] = turn
+
         @pl.when(turn == 0)
         def _():
-            pass_on(B_AT + 1, chain_b, has_down_b)
-            pass_on(A_AT + 1, chain_a, has_down_a)
+            pass_on(B_AT + 1, chain_b(1), has_down_b)
+            pass_on(A_AT + 1, chain_a(1), has_down_a)
             other_half(B_AT)
             other_half(A_AT)
             other_half(B_AT + 1, other)
 
         @pl.when(turn == 1)
         def _():
-            pass_on(B_AT + 4)
-            pass_on(B_AT + 3)
-            pass_on(A_AT + 3)
-            other_half(A_AT + 1, same)
+            when(near, second_blocks)
+            when(plain, far_blocks)
+            other_half(A_AT + 1, either(same, near))
             other_half(B_AT + 1, same)
-            other_half(A_AT + 3, other)
-            other_half(B_AT + 3, other)
-            other_half(B_AT + 4, other)
+            other_half(B_AT + 2, near_other)
+            other_half(A_AT + 3, plain_other)
+            other_half(B_AT + 3, plain_other)
+            other_half(B_AT + 4, plain_other)
 
         @pl.when(turn == 2)
         def _():
-            g_core(B_AT + 4).start()
-            pass_on(B_AT + 2)
-            pass_on(A_AT + 2)
-            other_half(A_AT + 3, same)
-            other_half(B_AT + 3, same)
-            other_half(A_AT + 2, either(other, alias_b))
-            other_half(B_AT + 2, other)
+            when(near, far_blocks)
+            when(plain, second_blocks)
+            other_half(A_AT + 3, plain_same)
+            other_half(B_AT + 3, either(plain_same, near_other))
+            other_half(A_AT + 2, either(other, alias_b, near))
+            other_half(B_AT + 2, either(plain_other, near_same))
 
         @pl.when(turn == 3)
         def _():
-            g_core(A_AT + 3).start()
-            g_core(B_AT + 3).start()
-            give_back(B_AT + 4, from_b4)
-            give_back(A_AT + 3, from_a3)
-            give_back(B_AT + 3, from_b3)
-            other_half(A_AT + 1, other)
-            other_half(A_AT + 2, both(same, jnp.logical_not(alias_b)))
-            other_half(B_AT + 2, same)
-
-        k = jnp.where(turn == 0, order[0], jnp.where(turn == 1, order[1], jnp.where(turn == 2, order[2], order[3])))
-        meeting(k)
-
+            when(plain, far_back)
+            other_half(A_AT + 1, plain_other)
+            other_half(A_AT + 2, both(plain_same, jnp.logical_not(alias_b)))
+            other_half(B_AT + 2, plain_same)
+            other_half(A_AT + 3, near)
+            other_half(B_AT + 3, near_same)
+            other_half(B_AT + 4, near_other)
+
+        meeting(in_turn(*order))
+
+    when(near, far_back)
     for k in (2, 1, 0):
         g_core(A_AT + k).start()
         g_core(B_AT + k).start()
@@ -339,8 +425,10 @@
             g[at, h] += returned[i]
 
     gathered(A_AT + 2)
+    chained(A_AT + 2, slot_a(2), send_a2)
     when(has_up_a, g_chain(A_AT + 2, up_a).start)
     gathered(B_AT + 2)
+    chained(B_AT + 2, slot_b(2), send_b2)
     when(has_up_b, g_chain(B_AT + 2, up_b).start)
     gathered(A_AT + 1)
     gathered(B_AT + 1)
@@ -360,7 +448,8 @@
 
     @pl.when(same)
     def _():
-        out[q] = g[A_AT, h]
+        for block in range(2):
+            when(q == block, functools.partial(lambda b: give(b, g[A_AT, h]), block))
 
     chained(B_AT, B_AT, has_down_b)
 
@@ -368,26 +457,31 @@
     def _():
         swap_out(1).start()
         swap_out(0).wait_recv()
-        out[1 - q] = swapped[0]
+        for block in range(2):
+            when(q == 1 - block, functools.partial(lambda b: give(b, swapped[0]), block))
         swap_out(1).wait_recv()
-        out[q] = swapped[1]
+        for block in range(2):
+            when(q == block, functools.partial(lambda b: give(b, swapped[1]), block))
 
     @pl.when(same)
     def _():
-        out[1 - q] = g[B_AT, h]
+        for block in range(2):
+            when(q == 1 - block, functools.partial(lambda b: give(b, g[B_AT, h]), block))
 
     @pl.when(is_fixed)
     def _():
         fixed_out.wait_recv()
-        out[0] += g[FIXED, q] + extra[...]
+        for group in range(groups):
+            lanes = pl.ds(group * LANES, LANES)
+            out[rows_of(0, group), :] += g[FIXED, q, :, lanes] + extra[:, lanes]
 
     other_half(B_AT + 4, same)
 
     @pl.when(other)
     def _():
-        for i in range(2):
-            swap_in(i).wait_send()
-            swap_out(i).wait_send()
+        swap_in.wait_send()
+        swap_out(0).wait_send()
+        swap_out(1).wait_send()
 
     when(fixed_giver, fixed_in.wait_send)
     when(is_fixed, fixed_out.wait_send)
@@ -396,6 +490,9 @@
     for k in range(2):
         when(has_down_a, chain_a(k).wait_send)
         when(has_down_b, chain_b(k).wait_send)
+    when(send_a2, chain_a(2).wait_send)
+    when(send_b2, chain_b(2).wait_send)
+    when(send_b3, chain_b(3).wait_send)
     for at in range(9):
         if at in has:
             when(has[at], to_core(at).wait_send)
@@ -405,9 +502,11 @@
     for k in (1, 2):
         when(has_up_a, g_chain(A_AT + k, up_a).wait_send)
         when(has_up_b, g_chain(B_AT + k, up_b).wait_send)
-    when(from_a3[0], g_return(A_AT + 3, from_a3).wait_send)
-    when(from_b3[0], g_return(B_AT + 3, from_b3).wait_send)
-    when(from_b4[0], g_return(B_AT + 4, from_b4).wait_send)
+    for at, source, present, up in (
+        (A_AT + 3, from_a3, has_up_a, up_a), (B_AT + 3, from_b3, has_b3, up_b), (B_AT + 4, from_b4, has_b4, up_b),
+    ):
+        when(source[0], g_return(at, source).wait_send)
+        when(both(present, jnp.logical_not(source[0])), g_chain(at, up).wait_send)
 
 
 def solution(mesh):
@@ -418,16 +517,19 @@
         share, items = factors.shape[2], factors.shape[3]
         tile = min(512, items)
         dma = pltpu.SemaphoreType.DMA
+        packed = pack(factors[0])
         grad = pl.pallas_call(
             functools.partial(kernel, chips, tile),
-            out_shape=jax.ShapeDtypeStruct((2, share, items), F32),
+            out_shape=jax.ShapeDtypeStruct(packed.shape, F32),
             in_specs=[pl.BlockSpec(memory_space=pl.ANY)] * 2,
             out_specs=pl.BlockSpec(memory_space=pltpu.VMEM),
             scratch_shapes=[
                 pltpu.VMEM((SLOTS, 2, share, items), F32),
                 pltpu.VMEM((SLOTS, 2, share, items), F32),
+                pltpu.VMEM(packed.shape, F32),
+                pltpu.VMEM(packed.shape, F32),
                 pltpu.VMEM((9, share, items), F32),
-                pltpu.VMEM((6, share, items), F32),
+                pltpu.VMEM((8, share, items), F32),
                 pltpu.VMEM((4, share, items), F32),
                 pltpu.VMEM((2, share, items), F32),
                 pltpu.VMEM((share, items), F32),
@@ -436,20 +538,19 @@
                 pltpu.VMEM((2, share, items), BF16),
                 pltpu.VMEM((2, share, items), BF16),
                 pltpu.VMEM((2, share, items), BF16),
-                dma((3,)), dma((4,)),
-                dma((2,)), dma((2,)), dma, dma,
-                dma((8,)), dma((9,)), dma((9,)), dma((9,)),
-                dma((9,)), dma((9,)), dma((9,)), dma((6,)), dma((4,)),
+                dma((2,)), dma((4,)),
+                dma, dma, dma, dma,
+                dma((11,)), dma((9,)), dma((9,)), dma((9,)),
+                dma((9,)), dma((9,)), dma((9,)), dma((8,)), dma((4,)),
                 dma((2,)), dma((2,)), dma, dma,
             ],
             compiler_params=pltpu.CompilerParams(
                 collective_id=0, has_side_effects=True, vmem_limit_bytes=60 * 1024 * 1024
             ),
-        )(factors[0], counts[0])
-        grad = grad[None]
-        new_state = state + grad * grad
+        )(packed, counts[0])
+        new_state = pack(state[0]) + grad * grad
         step = grad / jnp.sqrt(new_state)
-        return (step, new_state)
+        return (unpack(step, factors.shape), unpack(new_state, factors.shape))
 
     in_specs = (
         P("blk", None, "rep", None),

time: 122 us -> 103 us (0.84)
  the two profiles are of different devices: /device:TPU:243 before, /device:TPU:211 now
where the time goes in v3:
time: 103 us
  Pallas kernels  99.8 us (97%)
  other arithmetic  2.18 us (2%)
    pallas_call x1, Pallas kernels, body(): pl.pallas_call(functools.partial(kernel, chips, tile), out_shape=jax.Shap...  99.8 us
    add x1, other arithmetic, body(): new_state = pack(state[0]) + grad * grad  2.18 us

profile of v3, /device:TPU:211, one launch (start us, length us, event | category | flops | bytes accessed | tf_op | source)
XLA Modules:
  0.0 102.7 jit_solution(3034005131540897219)
XLA Ops:
  0.6 0.0 copy-start
  0.6 99.8 %shard_map.50 = f32[1200,128]{1,0:T(8,128)} custom-call(f32[1200,128]{1,0:T(8,128)} %bitcast.25, s32[8,512,512]{2,1,0:T(8,128)} %bitcast.21), custom_call_target="tpu_custom_call" | custom-call | tf_op jit(solution)/shard_map/pallas_call | solution.py:521
  100.5 0.0 copy-done
  100.5 2.2 %multiply_add_fusion = (f32[1200,128]{1,0:T(8,128)}, f32[1200,128]{1,0:T(8,128)}) fusion(f32[1200,128]{1,0:T(8,128)S(1)} %bitcast.22, f32[1200,128]{1,0:T(8,128)} %shard_map.50), kind=kLoop, calls=%fused_computation.1 | loop fusion | flops 460800 | bytes 2457600 | tf_op jit(solution)/shard_map/add | solution.py:551
Async XLA Ops:
  0.6 99.8 %copy-start = (f32[1,2,150,512]{3,1,2,0:T(2,128)S(1)}, f32[1,2,150,512]{3,1,2,0:T(2,128)}, u32[]{:S(2)}) copy-start(f32[1,2,150,512]{3,1,2,0:T(2,128)} %param.4) | copy-start | bytes 1843204

commit v4 on v3

--- a/solution.py
+++ b/solution.py
@@ -30,13 +30,8 @@
     return high, (value - high.astype(F32)).astype(BF16)
 
 
-def dot3(left, right, dims):
-    (lh, ll), (rh, rl) = left, right
-
-    def one(a, b):
-        return lax.dot_general(a, b, (dims, ((), ())), preferred_element_type=F32)
-
-    return one(lh, rh) + one(lh, rl) + one(ll, rh)
+def product(left, right, dims):
+    return lax.dot_general(left, right, (dims, ((), ())), preferred_element_type=F32)
 
 
 def pack(blocks):
@@ -50,8 +45,8 @@
 
 
 def kernel(
-    chips, tile, factors, counts, out,
-    x, g, raw, mine, from_core, from_chain, returned, swapped, extra, tiles, uh, ul, lh, ll,
+    chips, factors, counts, out,
+    x, g, raw, mine, from_core, from_chain, returned, swapped, extra, tiles, upper_parts, lower_parts, lower_twice,
     load_sem, count_sem,
     in_send, in_recv, fix_send, fix_recv,
     out_block_send, block_recv, core_send, core_recv,
@@ -96,10 +91,10 @@
     half_way = chips // 2
 
     def right_fed(chip):
-        return both(chip >= half_way, chip < half_way + 3)
+        return both(chip > half_way, chip < half_way + 3)
 
     def left_fed(chip):
-        return either(both(chip >= half_way - 3, chip < half_way), chip >= chips - 3)
+        return both(chip >= half_way - 3, chip < half_way - 1)
 
     def fed_a3(to):
         return jnp.where(to[1] == 0, right_fed(to[0] // 2), left_fed(to[0] // 2))
@@ -110,8 +105,17 @@
     def fed_b4(to):
         return both(to[1] == 0, to[0] // 2 == chips - 4)
 
+    def home_of(to):
+        stays = to[1] == h
+        return (jnp.where(stays, to[0], to[0] // 2 * 2 + 1 - h), jnp.where(stays, to[1], 1 - to[1]))
+
+    over = c + 1 >= chips
+    partner_right = (jnp.where(over, c, c + 1) * 2 + 1 - h, jnp.where(over, q, 1 - q))
+    partner_left = (jnp.maximum(c - 1, 0) * 2 + 1 - h, 1 - q)
+    last_a_from, last_b_from = pick(odd, partner_right, partner_left), pick(odd, partner_left, partner_right)
+    alias_home = both(odd, c == 0)
     here = (p, q)
-    near = either(both(c >= half_way - 3, c < half_way + 3), c >= chips - 4)
+    near = both(c >= half_way - 3, c < half_way + 3)
     plain = jnp.logical_not(near)
     send_a2, send_b2 = both(has_down_a, fed_a3(down_a)), both(has_down_b, fed_b3(down_b))
     send_b3 = both(has_down_b, fed_b4(down_b))
@@ -237,6 +241,13 @@
         *[(f[0], f[1]) for f in far], from_a3[:2], from_b3[:2], from_b4[:2],
     ]
     greeted = 0
+    for condition, to in ((both(other, has_up_a), last_a_from), (both(other, has_up_b), last_b_from)):
+        @pl.when(condition)
+        def _(to=to):
+            pl.semaphore_signal(barrier, inc=1, device_id=to, device_id_type=MESH)
+
+    for condition, up in ((has_up_a, up_a), (has_up_b, up_b)):
+        greeted += jnp.where(both(condition, up[1] != h), 1, 0)
     for condition, to in peers:
         def greet(to=to):
             pl.semaphore_signal(barrier, inc=1, device_id=to, device_id_type=MESH)
@@ -250,10 +261,6 @@
     pl.semaphore_wait(barrier, greeted)
 
     when(other, swap_in.start)
-
-    @pl.loop(0, SLOTS)
-    def _(at):
-        g[at] = jnp.zeros_like(g[at])
 
     when(either(same, fixed_taker), own.wait)
     for source, condition in ((mine, same), (raw, other)):
@@ -272,6 +279,16 @@
         when(far[i][0], far_block(i).start)
     when(fixed_giver, fixed_in.start)
 
+    @pl.loop(0, SLOTS)
+    def _(at):
+        g[at] = jnp.zeros_like(g[at])
+
+    padded = upper_parts.shape[0] // 4
+    if padded > share:
+        for parts in (upper_parts, lower_parts):
+            for i in range(4):
+                parts[pl.ds(i * padded + share, padded - share), :] = jnp.zeros((padded - share, items), BF16)
+
     @pl.when(fixed_taker)
     def _():
         take(mine, 0, FIXED, 1)
@@ -283,19 +300,28 @@
         lower = jnp.where(even, b, a)
         g_upper = jnp.where(is_fixed, FIXED, upper)
         counts_in(k).wait()
-        for half in range(2):
-            uh[half], ul[half] = split(x[upper, half])
-            lh[half], ll[half] = split(x[lower, half])
-
-        for start in range(0, items, tile):
-            rows = pl.ds(start, tile)
-            scores = 0.0
+        for parts, at in ((upper_parts, upper), (lower_parts, lower)):
             for half in range(2):
-                scores += dot3((uh[half, :, rows], ul[half, :, rows]), (lh[half], ll[half]), ((0,), (0,)))
-            r = split(residual_of(scores, tiles[k, rows, :]))
+                high, low = split(x[at, half])
+                parts[pl.ds(half * padded, share), :] = high
+                parts[pl.ds((2 + half) * padded, share), :] = low
+        lower_twice[: 2 * padded] = lower_parts[: 2 * padded]
+        lower_twice[2 * padded :] = lower_parts[: 2 * padded]
+        over_features = ((0,), (0,))
+        scores = product(upper_parts[...], lower_twice[...], over_features) + product(
+            upper_parts[: 2 * padded], lower_parts[2 * padded :], over_features
+        )
+        r_high, r_low = split(residual_of(scores, tiles[k]))
+
+        def add_to(at, parts, dims):
+            first = product(parts[...], r_high, dims)
+            second = product(parts[: 2 * padded], r_low, dims)
             for half in range(2):
-                g[lower, half] += dot3((uh[half, :, rows], ul[half, :, rows]), r, ((1,), (0,)))
-                g[g_upper, half, :, rows] += dot3((lh[half], ll[half]), r, ((1,), (1,)))
+                i, j = half * padded, (2 + half) * padded
+                g[at, half] += first[i : i + share] + first[j : j + share] + second[i : i + share]
+
+        add_to(lower, upper_parts, ((1,), (0,)))
+        add_to(g_upper, lower_parts, ((1,), (1,)))
 
     has = {1: has_up_a, 2: has_up_a, 3: has_up_a, 5: has_up_b, 6: has_up_b, 7: has_b3, 8: has_b4}
 
@@ -430,41 +456,50 @@
     gathered(B_AT + 2)
     chained(B_AT + 2, slot_b(2), send_b2)
     when(has_up_b, g_chain(B_AT + 2, up_b).start)
+    gathered(A_AT)
+    gathered(B_AT)
+    chained(B_AT + 1, slot_b(1), alias_b)
+    for i in (0, 1, 2, 3):
+        add_returned(i, far[i][2])
+
+    @pl.when(other)
+    def _():
+        swap_out(0).start()
+        swap_out(1).start()
+
     gathered(A_AT + 1)
     gathered(B_AT + 1)
     chained(A_AT + 1, slot_a(1), has_down_a)
-    when(has_up_a, g_chain(A_AT + 1, up_a).start)
-    chained(B_AT + 1, slot_b(1), has_down_b)
-    when(has_up_b, g_chain(B_AT + 1, up_b).start)
-    gathered(A_AT)
-    gathered(B_AT)
-    for i in (0, 1, 2, 3):
-        add_returned(i, far[i][2])
-    chained(A_AT, slot_a(0), has_down_a)
-
+    when(has_up_a, g_chain(A_AT + 1, home_of(up_a)).start)
+    chained(B_AT + 1, B_AT + 1, both(has_down_b, jnp.logical_not(alias_b)))
+    when(has_up_b, g_chain(B_AT + 1, home_of(up_b)).start)
     @pl.when(other)
     def _():
-        swap_out(0).start()
+        swap_out(0).wait_recv()
+        swap_out(1).wait_recv()
+
+        @pl.when(has_up_a)
+        def _():
+            g_chain_arrival(A_AT).wait_recv()
+            swapped[jnp.where(alias_home, 1, 0)] += from_chain[A_AT]
+
+        for block in range(2):
+            when(q == 1 - block, functools.partial(lambda b: give(b, swapped[0]), block))
+
+        @pl.when(has_up_b)
+        def _():
+            g_chain_arrival(B_AT).wait_recv()
+            swapped[1] += from_chain[B_AT]
+
+        for block in range(2):
+            when(q == block, functools.partial(lambda b: give(b, swapped[1]), block))
 
     @pl.when(same)
     def _():
+        chained(A_AT, slot_a(0), has_down_a)
         for block in range(2):
             when(q == block, functools.partial(lambda b: give(b, g[A_AT, h]), block))
-
-    chained(B_AT, B_AT, has_down_b)
-
-    @pl.when(other)
-    def _():
-        swap_out(1).start()
-        swap_out(0).wait_recv()
-        for block in range(2):
-            when(q == 1 - block, functools.partial(lambda b: give(b, swapped[0]), block))
-        swap_out(1).wait_recv()
-        for block in range(2):
-            when(q == block, functools.partial(lambda b: give(b, swapped[1]), block))
-
-    @pl.when(same)
-    def _():
+        chained(B_AT, B_AT, has_down_b)
         for block in range(2):
             when(q == 1 - block, functools.partial(lambda b: give(b, g[B_AT, h]), block))
 
@@ -500,8 +535,8 @@
             to_core(at).wait_send()
         g_core(at).wait_send()
     for k in (1, 2):
-        when(has_up_a, g_chain(A_AT + k, up_a).wait_send)
-        when(has_up_b, g_chain(B_AT + k, up_b).wait_send)
+        when(has_up_a, g_chain(A_AT + k, home_of(up_a) if k == 1 else up_a).wait_send)
+        when(has_up_b, g_chain(B_AT + k, home_of(up_b) if k == 1 else up_b).wait_send)
     for at, source, present, up in (
         (A_AT + 3, from_a3, has_up_a, up_a), (B_AT + 3, from_b3, has_b3, up_b), (B_AT + 4, from_b4, has_b4, up_b),
     ):
@@ -515,11 +550,11 @@
 
     def body(factors, state, counts):
         share, items = factors.shape[2], factors.shape[3]
-        tile = min(512, items)
+        padded = -(-share // 16) * 16
         dma = pltpu.SemaphoreType.DMA
         packed = pack(factors[0])
         grad = pl.pallas_call(
-            functools.partial(kernel, chips, tile),
+            functools.partial(kernel, chips),
             out_shape=jax.ShapeDtypeStruct(packed.shape, F32),
             in_specs=[pl.BlockSpec(memory_space=pl.ANY)] * 2,
             out_specs=pl.BlockSpec(memory_space=pltpu.VMEM),
@@ -534,10 +569,9 @@
                 pltpu.VMEM((2, share, items), F32),
                 pltpu.VMEM((share, items), F32),
                 pltpu.VMEM((4, items, items), jnp.int32),
-                pltpu.VMEM((2, share, items), BF16),
-                pltpu.VMEM((2, share, items), BF16),
-                pltpu.VMEM((2, share, items), BF16),
-                pltpu.VMEM((2, share, items), BF16),
+                pltpu.VMEM((4 * padded, items), BF16),
+                pltpu.VMEM((4 * padded, items), BF16),
+                pltpu.VMEM((4 * padded, items), BF16),
                 dma((2,)), dma((4,)),
                 dma, dma, dma, dma,
                 dma((11,)), dma((9,)), dma((9,)), dma((9,)),

time: 103 us -> 94 us (0.913)
  the two profiles are of different devices: /device:TPU:211 before, /device:TPU:243 now
where the time goes in v4:
time: 94 us; the launch traced here: 92.5 us
  Pallas kernels  89.6 us (95%)
  other arithmetic  2.18 us (2%)
    pallas_call x1, Pallas kernels, body(): pl.pallas_call(functools.partial(kernel, chips), out_shape=jax.ShapeDtype...  89.6 us
    add x1, other arithmetic, body(): new_state = pack(state[0]) + grad * grad  2.18 us

profile of v4, /device:TPU:243, one launch (start us, length us, event | category | flops | bytes accessed | tf_op | source)
XLA Modules:
  0.0 92.5 jit_solution(9577467060828706947)
XLA Ops:
  0.6 0.0 copy-start
  0.6 89.6 %shard_map.50 = f32[1200,128]{1,0:T(8,128)} custom-call(f32[1200,128]{1,0:T(8,128)} %bitcast.25, s32[8,512,512]{2,1,0:T(8,128)} %bitcast.21), custom_call_target="tpu_custom_call" | custom-call | tf_op jit(solution)/shard_map/pallas_call | solution.py:556
  90.3 0.0 copy-done
  90.3 2.2 %multiply_add_fusion = (f32[1200,128]{1,0:T(8,128)}, f32[1200,128]{1,0:T(8,128)}) fusion(f32[1200,128]{1,0:T(8,128)S(1)} %bitcast.22, f32[1200,128]{1,0:T(8,128)} %shard_map.50), kind=kLoop, calls=%fused_computation.1 | loop fusion | flops 460800 | bytes 2457600 | tf_op jit(solution)/shard_map/add | solution.py:585
Async XLA Ops:
  0.6 89.7 %copy-start = (f32[1,2,150,512]{3,1,2,0:T(2,128)S(1)}, f32[1,2,150,512]{3,1,2,0:T(2,128)}, u32[]{:S(2)}) copy-start(f32[1,2,150,512]{3,1,2,0:T(2,128)} %param.4) | copy-start | bytes 1843204

commit v5 on v4

--- a/solution.py
+++ b/solution.py
@@ -46,9 +46,9 @@
 
 def kernel(
     chips, factors, counts, out,
-    x, g, raw, mine, from_core, from_chain, returned, swapped, extra, tiles, upper_parts, lower_parts, lower_twice,
+    x, g, raw, mine, spare, from_core, from_chain, returned, swapped, extra, tiles, upper_parts, lower_parts, lower_twice,
     load_sem, count_sem,
-    in_send, in_recv, fix_send, fix_recv,
+    in_send, in_recv, fix_send, fix_recv, hold_send,
     out_block_send, block_recv, core_send, core_recv,
     gcore_send, gcore_recv, gback_send, gchain_recv, returned_recv,
     out_send, out_recv, gfix_send, gfix_recv,
@@ -187,6 +187,27 @@
     def from_core_arrival(at):
         return remote(x.at[at, 1 - h], x.at[at, 1 - h], core_send.at[at], core_recv.at[at], sibling)
 
+    holder = both(other, c >= chips - 4)
+
+    def held(j):
+        slot = (jnp.where(odd, A_AT + 1, B_AT + 1), jnp.where(odd, A_AT + 3, B_AT + 3), B_AT + 4)[j]
+        chip = (c, 2 * chips - 4 - c, 2 * chips - 5 - c)[j]
+        to = (jnp.clip(chip, 0, chips - 1) * 2 + 1 - h, q)
+        return remote(spare, x.at[slot, 1 - h], hold_send.at[j], block_recv.at[slot], to)
+
+    holds = (
+        both(holder, c == chips - 1),
+        both(holder, c >= chips - 3),
+        both(holder, even, c <= chips - 2),
+    )
+    takes_held = (
+        (both(same, c >= chips - 3), (jnp.clip(2 * chips - 4 - c, 0, chips - 1) * 2 + 1 - h, q)),
+        (both(same, even, c >= chips - 3), (jnp.clip(2 * chips - 5 - c, 0, chips - 1) * 2 + 1 - h, q)),
+    )
+
+    def sends(condition, to):
+        return both(condition, jnp.logical_not(both(other, to[1] != q)))
+
     def g_core(at):
         return remote(g.at[at, 1 - h], from_core.at[at], gcore_send.at[at], gcore_recv.at[at], sibling)
 
@@ -231,7 +252,7 @@
         for group in range(groups):
             out[rows_of(block, group), :] = value[:, group * LANES : (group + 1) * LANES]
 
-    when(either(same, fixed_taker), own.start)
+    when(either(same, fixed_taker, holder), own.start)
     for k in range(4):
         counts_in(k).start()
 
@@ -246,6 +267,12 @@
         def _(to=to):
             pl.semaphore_signal(barrier, inc=1, device_id=to, device_id_type=MESH)
 
+    for condition, to in takes_held:
+        @pl.when(condition)
+        def _(to=to):
+            pl.semaphore_signal(barrier, inc=1, device_id=to, device_id_type=MESH)
+
+    greeted += jnp.where(holds[1], 1, 0) + jnp.where(holds[2], 1, 0)
     for condition, up in ((has_up_a, up_a), (has_up_b, up_b)):
         greeted += jnp.where(both(condition, up[1] != h), 1, 0)
     for condition, to in peers:
@@ -262,7 +289,15 @@
 
     when(other, swap_in.start)
 
-    when(either(same, fixed_taker), own.wait)
+    when(either(same, fixed_taker, holder), own.wait)
+
+    @pl.when(holder)
+    def _():
+        for group in range(groups):
+            spare[:, pl.ds(group * LANES, LANES)] = mine[rows_of(0, group), :]
+        for j in range(3):
+            when(holds[j], held(j).start)
+
     for source, condition in ((mine, same), (raw, other)):
         @pl.when(condition)
         def _(source=source):
@@ -271,12 +306,19 @@
             for block in range(2):
                 take(source, block, jnp.where(q == block, A_AT, B_AT), h)
 
-    when(has_down_b, chain_b(0).start)
-    when(has_down_a, chain_a(0).start)
+    when(sends(has_down_b, down_b), chain_b(0).start)
+    when(sends(has_down_a, down_a), chain_a(0).start)
     to_core(B_AT).start()
     to_core(A_AT).start()
-    for i in (1, 0, 2, 3):
-        when(far[i][0], far_block(i).start)
+    def crossing(to):
+        return (to[0] // 2 >= half_way) != (c >= half_way)
+
+    def send_far(late):
+        for i in (1, 0, 2, 3):
+            crosses = crossing(far[i][1])
+            when(both(sends(*far[i][:2]), crosses if late else jnp.logical_not(crosses)), far_block(i).start)
+
+    send_far(False)
     when(fixed_giver, fixed_in.start)
 
     @pl.loop(0, SLOTS)
@@ -398,6 +440,7 @@
             pass_on(A_AT + 1, chain_a(1), has_down_a)
             other_half(B_AT)
             other_half(A_AT)
+            send_far(True)
             other_half(B_AT + 1, other)
 
         @pl.when(turn == 1)
@@ -519,12 +562,14 @@
         swap_out(1).wait_send()
 
     when(fixed_giver, fixed_in.wait_send)
+    for j in range(3):
+        when(holds[j], held(j).wait_send)
     when(is_fixed, fixed_out.wait_send)
     for i in range(4):
-        when(far[i][0], far_block(i).wait_send)
+        when(sends(*far[i][:2]), far_block(i).wait_send)
     for k in range(2):
-        when(has_down_a, chain_a(k).wait_send)
-        when(has_down_b, chain_b(k).wait_send)
+        when(sends(has_down_a, down_a) if k == 0 else has_down_a, chain_a(k).wait_send)
+        when(sends(has_down_b, down_b) if k == 0 else has_down_b, chain_b(k).wait_send)
     when(send_a2, chain_a(2).wait_send)
     when(send_b2, chain_b(2).wait_send)
     when(send_b3, chain_b(3).wait_send)
@@ -563,6 +608,7 @@
                 pltpu.VMEM((SLOTS, 2, share, items), F32),
                 pltpu.VMEM(packed.shape, F32),
                 pltpu.VMEM(packed.shape, F32),
+                pltpu.VMEM((share, items), F32),
                 pltpu.VMEM((9, share, items), F32),
                 pltpu.VMEM((8, share, items), F32),
                 pltpu.VMEM((4, share, items), F32),
@@ -573,7 +619,7 @@
                 pltpu.VMEM((4 * padded, items), BF16),
                 pltpu.VMEM((4 * padded, items), BF16),
                 dma((2,)), dma((4,)),
-                dma, dma, dma, dma,
+                dma, dma, dma, dma, dma((3,)),
                 dma((11,)), dma((9,)), dma((9,)), dma((9,)),
                 dma((9,)), dma((9,)), dma((9,)), dma((8,)), dma((4,)),
                 dma((2,)), dma((2,)), dma, dma,

time: 94 us -> 93 us (0.989); the launches traced: 92.5 us -> 92.9 us
  no operation moved by 1% of the time
where the time goes in v5:
time: 93 us; the launch traced here: 92.9 us
  Pallas kernels  90 us (97%)
  other arithmetic  2.18 us (2%)
    pallas_call x1, Pallas kernels, body(): pl.pallas_call(functools.partial(kernel, chips), out_shape=jax.ShapeDtype...  90 us
    add x1, other arithmetic, body(): new_state = pack(state[0]) + grad * grad  2.18 us

profile of v5, /device:TPU:243, one launch (start us, length us, event | category | flops | bytes accessed | tf_op | source)
XLA Modules:
  0.0 92.9 jit_solution(17383403746491593987)
XLA Ops:
  0.6 0.0 copy-start
  0.6 90.0 %shard_map.50 = f32[1200,128]{1,0:T(8,128)} custom-call(f32[1200,128]{1,0:T(8,128)} %bitcast.25, s32[8,512,512]{2,1,0:T(8,128)} %bitcast.21), custom_call_target="tpu_custom_call" | custom-call | tf_op jit(solution)/shard_map/pallas_call | solution.py:601
  90.7 0.0 copy-done
  90.7 2.2 %multiply_add_fusion = (f32[1200,128]{1,0:T(8,128)}, f32[1200,128]{1,0:T(8,128)}) fusion(f32[1200,128]{1,0:T(8,128)S(1)} %bitcast.22, f32[1200,128]{1,0:T(8,128)} %shard_map.50), kind=kLoop, calls=%fused_computation.1 | loop fusion | flops 460800 | bytes 2457600 | tf_op jit(solution)/shard_map/add | solution.py:631
Async XLA Ops:
  0.6 90.1 %copy-start = (f32[1,2,150,512]{3,1,2,0:T(2,128)S(1)}, f32[1,2,150,512]{3,1,2,0:T(2,128)}, u32[]{:S(2)}) copy-start(f32[1,2,150,512]{3,1,2,0:T(2,128)} %param.4) | copy-start | bytes 1843204

commit v6 on v5

--- a/solution.py
+++ b/solution.py
@@ -160,8 +160,8 @@
             src_ref=src, dst_ref=dst, send_sem=send, recv_sem=recv, device_id=to, device_id_type=MESH
         )
 
-    own = pltpu.make_async_copy(factors, mine, load_sem.at[0])
-    swap_in = remote(factors, raw, in_send, in_recv, partner)
+    own = pltpu.make_async_copy(factors, mine.at[pl.ds(0, factors.shape[0])], load_sem.at[0])
+    swap_in = remote(factors, raw.at[pl.ds(0, factors.shape[0])], in_send, in_recv, partner)
 
     def counts_in(k):
         return pltpu.make_async_copy(counts.at[2 * k + differs], tiles.at[k], count_sem.at[k])
@@ -598,16 +598,17 @@
         padded = -(-share // 16) * 16
         dma = pltpu.SemaphoreType.DMA
         packed = pack(factors[0])
+        room = -(-share // 8) * 8 * 2 * items // LANES
         grad = pl.pallas_call(
             functools.partial(kernel, chips),
-            out_shape=jax.ShapeDtypeStruct(packed.shape, F32),
+            out_shape=jax.ShapeDtypeStruct((room, LANES), F32),
             in_specs=[pl.BlockSpec(memory_space=pl.ANY)] * 2,
             out_specs=pl.BlockSpec(memory_space=pltpu.VMEM),
             scratch_shapes=[
                 pltpu.VMEM((SLOTS, 2, share, items), F32),
                 pltpu.VMEM((SLOTS, 2, share, items), F32),
-                pltpu.VMEM(packed.shape, F32),
-                pltpu.VMEM(packed.shape, F32),
+                pltpu.VMEM((room, LANES), F32),
+                pltpu.VMEM((room, LANES), F32),
                 pltpu.VMEM((share, items), F32),
                 pltpu.VMEM((9, share, items), F32),
                 pltpu.VMEM((8, share, items), F32),
@@ -628,6 +629,7 @@
                 collective_id=0, has_side_effects=True, vmem_limit_bytes=60 * 1024 * 1024
             ),
         )(packed, counts[0])
+        grad = grad[: packed.shape[0]]
         new_state = pack(state[0]) + grad * grad
         step = grad / jnp.sqrt(new_state)
         return (unpack(step, factors.shape), unpack(new_state, factors.shape))

time: 93 us -> 93 us (level)
    add x1 -> x0, other arithmetic: 2.18 us -> none  [body(): new_state = pack(state[0]) + grad * grad]
    div x0 -> x1, other arithmetic: none -> 2.18 us  [body(): step = grad / jnp.sqrt(new_state)]
where the time goes in v6:
time: 93 us; the launch traced here: 92.9 us
  Pallas kernels  90 us (97%)
  other arithmetic  2.18 us (2%)
    pallas_call x1, Pallas kernels, body(): pl.pallas_call(functools.partial(kernel, chips), out_shape=jax.ShapeDtype...  90 us
    div x1, other arithmetic, body(): step = grad / jnp.sqrt(new_state)  2.18 us

profile of v6, /device:TPU:243, one launch (start us, length us, event | category | flops | bytes accessed | tf_op | source)
XLA Modules:
  0.0 92.9 jit_solution(688707504648269970)
XLA Ops:
  0.6 0.0 copy-start
  0.6 90.0 %shard_map.50 = f32[1216,128]{1,0:T(8,128)} custom-call(f32[1200,128]{1,0:T(8,128)} %bitcast.25, s32[8,512,512]{2,1,0:T(8,128)} %bitcast.21), custom_call_target="tpu_custom_call" | custom-call | tf_op jit(solution)/shard_map/pallas_call | solution.py:602
  90.7 0.0 copy-done
  90.7 2.2 %rsqrt_multiply_fusion = (f32[1200,128]{1,0:T(8,128)}, f32[1200,128]{1,0:T(8,128)}) fusion(f32[1216,128]{1,0:T(8,128)} %shard_map.50, f32[1200,128]{1,0:T(8,128)S(1)} %bitcast.22), kind=kLoop, calls=%fused_computation | loop fusion | flops 460800 | bytes 2457600 | tf_op jit(solution)/shard_map/div | solution.py:634
Async XLA Ops:
  0.6 90.0 %copy-start = (f32[1,2,150,512]{3,1,2,0:T(2,128)S(1)}, f32[1,2,150,512]{3,1,2,0:T(2,128)}, u32[]{:S(2)}) copy-start(f32[1,2,150,512]{3,1,2,0:T(2,128)} %param.4) | copy-start | bytes 1843204
